TPU v7x, 128 devices: a whole 4x4x4 slice. The times are simulated.
128 devices in a mesh: expert: 64 (over y, z, x), half: 2 (over core).
Axes of the slice: x: 4, y: 4, z: 4, core: 2. Of those that a mesh axis runs over, the one named last changes fastest.
Arguments:
- hidden_in: bfloat16 [8192, 2048], P('expert'), may hold values from -6 to 6
- modality: int32 [8192], replicated, may hold values from 0 to 1, as said below
- expert_ids: int32 [8192, 8], P('expert'), may hold values from 0 to 63, all different within a row; in each aligned block of 128 rows (0 to 127, 128 to 255, ...) at most 24 rows name the same one
- route_weights: float32 [8192, 8], P('expert'), may hold values from 0.03 to 0.3
- w_gate_up: bfloat16 [128, 2048, 2, 768], P('expert', None, None, 'half'), may hold values from -0.125 to 0.125
- w_down: bfloat16 [128, 768, 2048], P('expert', 'half'), may hold values from -0.21875 to 0.21875
- norm_gain: float32 [2048], replicated, may hold values from 0.1 to 1.9
- w_query: bfloat16 [2048, 4096], P(None, 'half'), may hold values from -1 to 1
- key_value_weight: bfloat16 [2048, 2, 512], P(None, None, 'half'), may hold values from -1 to 1
- q_gain: float32 [128], replicated, may hold values from 1 to 8
- k_gain: float32 [128], replicated, may hold values from 1 to 8
Outputs:
- hidden_out: float32 [8192, 2048], P('expert')
- attended: bfloat16 [8192, 4096], P('expert', 'half')
Inputs may be any that keep to these rules, and one draw needn't show every extreme that they name: `modality`: constant over each aligned block of 128 tokens; both values occur. `expert_ids`: the 8 ids of a token differ; among the tokens of one aligned block of 128 no id is named more than 24 times, a bound that some block reaches.
All inputs are finite; a program needn't handle non-finite values.
Results may differ from a plain program's by a relative error of at most 0.03.
The roundings to bfloat16 on the way count: a program that leaves them out, or rounds other values in their place, can miss the bound.
Values may be sent and summed in bfloat16 or wider, within the bound.
A program may use at most 128 MiB of HBM per device.

v0:
```python
import math

import jax
import jax.numpy as jnp
from jax import lax
from jax.sharding import PartitionSpec as P

EPSILON = 1e-06


def from_partner(block, axis, stride):
    count = lax.axis_size(axis)
    route = []
    for low in range(count):
        high = low | 1 << stride
        if high != low and high < count:
            route += [(low, high), (high, low)]
    return lax.ppermute(block, axis, route)


def rms_scale(values, gain_row):
    mean_sq = jnp.mean(values * values, axis=-1, keepdims=True)
    return values * lax.rsqrt(mean_sq + EPSILON) * gain_row


def expert_pass(received, source_kind, w_gate_up, w_down):
    groups, slots, model_width = received.shape
    ordering = jnp.argsort(source_kind, stable=True)
    restore = jnp.argsort(ordering, stable=True)
    text_count = jnp.sum((source_kind == 0).astype(jnp.int32))
    group_sizes = jnp.stack([text_count * slots, (groups - text_count) * slots])
    rows_sorted = received[ordering].reshape(groups * slots, model_width)
    local_experts = w_gate_up.shape[0]
    half_units = w_gate_up.shape[3]
    gate_up = lax.ragged_dot(
        rows_sorted,
        w_gate_up.reshape(local_experts, model_width, 2 * half_units),
        group_sizes,
        preferred_element_type=jnp.float32,
    )
    activated = (jax.nn.silu(gate_up[:, :half_units]) * gate_up[:, half_units:]).astype(
        jnp.bfloat16
    )
    partial_out = lax.ragged_dot(activated, w_down, group_sizes, preferred_element_type=jnp.float32)
    return partial_out.reshape(groups, slots, model_width)[restore]


def body(
    hidden_in,
    modality,
    expert_ids,
    route_weights,
    w_gate_up,
    w_down,
    norm_gain,
    w_query,
    key_value_weight,
    q_gain,
    k_gain,
):
    tok_rows, model_width = hidden_in.shape
    top_count = expert_ids.shape[1]
    groups = lax.axis_size("expert")
    capacity = max(2, 3 * tok_rows * top_count // (2 * groups))
    source_kind = modality.reshape(groups, tok_rows)[:, 0]
    flat_ids = expert_ids.reshape(-1)
    row_total = tok_rows * top_count
    one_hot = (flat_ids[:, None] == jnp.arange(groups, dtype=jnp.int32)[None, :]).astype(jnp.int32)
    slot_rank = jnp.sum((jnp.cumsum(one_hot, axis=0) - one_hot) * one_hot, axis=1)
    slot_index = flat_ids * capacity + slot_rank
    row_token = jnp.arange(row_total, dtype=jnp.int32) // top_count
    slot_token = jnp.full((groups * capacity,), tok_rows, jnp.int32).at[slot_index].set(row_token)
    padded_in = jnp.concatenate([hidden_in, jnp.zeros((1, model_width), hidden_in.dtype)], axis=0)
    outgoing = padded_in[slot_token].reshape(groups, capacity, model_width)
    partial_out = expert_pass(
        lax.all_to_all(outgoing, "expert", split_axis=0, concat_axis=0, tiled=True),
        source_kind,
        w_gate_up,
        w_down,
    )
    combined = partial_out + from_partner(partial_out, "half", 0)
    returned = lax.all_to_all(
        combined.astype(jnp.bfloat16), "expert", split_axis=0, concat_axis=0, tiled=True
    )
    part_width = returned.shape[2]
    gathered = (
        returned.reshape(groups * capacity, part_width)[slot_index]
        .astype(jnp.float32)
        .reshape(tok_rows, top_count, part_width)
    )
    mixture = jnp.sum(gathered * route_weights[:, :, None], axis=1)
    hidden_out = hidden_in.astype(jnp.float32) + mixture
    normalized_input = rms_scale(hidden_out, norm_gain).astype(jnp.bfloat16)
    head_dim = q_gain.shape[0]
    queries = jnp.dot(normalized_input, w_query, preferred_element_type=jnp.float32)
    local_heads = queries.shape[1] // head_dim
    queries = rms_scale(queries.reshape(tok_rows, local_heads, head_dim), q_gain).astype(
        jnp.bfloat16
    )
    kv_width = key_value_weight.shape[2]
    kv_heads = kv_width // head_dim
    key_value_rows = jnp.dot(
        normalized_input,
        key_value_weight.reshape(model_width, 2 * kv_width),
        preferred_element_type=jnp.float32,
    ).reshape(tok_rows, 2, kv_heads, head_dim)
    keys_local = rms_scale(key_value_rows[:, 0], k_gain).astype(jnp.bfloat16)
    values_local = key_value_rows[:, 1].astype(jnp.bfloat16)
    stacked = jnp.stack([keys_local, values_local], axis=1).reshape(tok_rows, 2, kv_width)
    queries_per_group = local_heads // kv_heads
    query_rows = queries_per_group * tok_rows
    grouped_queries = (
        queries.reshape(tok_rows, kv_heads, queries_per_group, head_dim)
        .transpose(1, 2, 0, 3)
        .reshape(kv_heads, query_rows, head_dim)
    )
    score_scale = head_dim ** (-0.5)
    initial = (
        jnp.full((kv_heads, query_rows), -1e30, jnp.float32),
        jnp.zeros((kv_heads, query_rows), jnp.float32),
        jnp.zeros((kv_heads, query_rows, head_dim), jnp.float32),
    )
    kv_piece = lax.all_gather(stacked, "expert", axis=0, tiled=True)
    key_rows = kv_piece.shape[0]
    key_block = math.gcd(key_rows, 1024)
    blocks = kv_piece.reshape(key_rows // key_block, key_block, 2, kv_heads, head_dim)

    def step_block(inner_state, kv_block):
        peak_in, totals_in, accum_in = inner_state
        scores = (
            jnp.einsum(
                "hrd,khd->hrk", grouped_queries, kv_block[:, 0], preferred_element_type=jnp.float32
            )
            * score_scale
        )
        new_peak = jnp.maximum(peak_in, jnp.max(scores, axis=-1))
        weights = jnp.exp(scores - new_peak[..., None])
        rescale = jnp.exp(peak_in - new_peak)
        totals_out = totals_in * rescale + jnp.sum(weights, axis=-1)
        accum_out = accum_in * rescale[..., None] + jnp.einsum(
            "hrk,khd->hrd",
            weights.astype(jnp.bfloat16),
            kv_block[:, 1],
            preferred_element_type=jnp.float32,
        )
        return ((new_peak, totals_out, accum_out), None)

    final_state = lax.scan(step_block, initial, blocks)[0]
    accumulated = final_state[2] / final_state[1][..., None]
    attended = (
        accumulated.reshape(kv_heads, queries_per_group, tok_rows, head_dim)
        .transpose(2, 0, 1, 3)
        .reshape(tok_rows, local_heads * head_dim)
        .astype(jnp.bfloat16)
    )
    return (hidden_out, attended)


def solution(mesh):
    in_specs = (
        P("expert", None),
        P(),
        P("expert", None),
        P("expert", None),
        P("expert", None, None, "half"),
        P("expert", "half", None),
        P(),
        P(None, "half"),
        P(None, None, "half"),
        P(),
        P(),
    )
    out_specs = (P("expert", None), P("expert", "half"))
    return jax.shard_map(body, mesh=mesh, in_specs=in_specs, out_specs=out_specs, check_vma=False)
```

profile of v0, /device:TPU:0, one launch (start us, length us, event | category | flops | bytes accessed | tf_op | source)
XLA Modules:
  0.0 563.3 jit_solution(2645386171560433740)
XLA Ops:
  8.9 18.0 %reduce-window.6 = s32[64,8,128]{2,1,0:T(8,128)S(1)} reduce-window(s32[64,8,128]{2,1,0:T(8,128)S(1)} %fusion.22, s32[]{:T(128)} %constant.32.clone.1), window={size=1x1x128 pad=0_0x0_0x127_0}, to_apply=%region_0.0 | reduce-window | flops 8323072 | bytes 524292 | tf_op jit(solution)/shard_map/reduce-window
  27.7 4.3 scatter_custom_fusion
  32.1 1.1 concatenate.4
  33.2 7.1 %gather_fusion = bf16[1536,2048]{1,0:T(8,128)(2,1)} fusion(bf16[129,2048]{1,0:T(8,128)(2,1)S(1)} %concatenate.4, s32[2048]{0:T(1024)S(1)} %pad_clamp_fusion), kind=kCustom, calls=%fused_computation | custom fusion | bytes 12589056 | tf_op jit(solution)/shard_map/gather | solution.py:74
  40.3 11.9 %all-to-all-start = ((bf16[64,24,2048]{2,1,0:T(8,128)(2,1)}), bf16[64,24,2048]{2,1,0:T(8,128)(2,1)}, u32[]{:S(2)}, u32[]{:S(2)}) async-start(bf16[64,24,2048]{2,1,0:T(8,128)(2,1)} %bitcast.107), calls=%async_computation | async-start | bytes 12582912 | tf_op jit(solution)/shard_map/all_to_all | solution.py:76
  52.3 2.0 sort.31
  56.8 1.3 ragged-dot-metadata
  58.2 14.6 %reshape.140 = bf16[2,2048,768]{2,1,0:T(8,128)(2,1)} reshape(bf16[2,2048,2,384]{3,2,1,0:T(2,128)(2,1)} %param.17) | data formatting | bytes 12582912 | tf_op jit(solution)/shard_map/reshape | solution.py:37
  72.8 2.0 sort.32
  74.8 57.0 %all-to-all-done = bf16[64,24,2048]{2,1,0:T(8,128)(2,1)} async-done(((bf16[64,24,2048]{2,1,0:T(8,128)(2,1)}), bf16[64,24,2048]{2,1,0:T(8,128)(2,1)}, u32[]{:S(2)}, u32[]{:S(2)}) %all-to-all-start) | async-done | bytes 6291488 | tf_op jit(solution)/shard_map/all_to_all | solution.py:76
  131.9 6.4 %gather_fusion.1 = bf16[64,24,2048]{2,1,0:T(8,128)(2,1)} fusion(bf16[64,24,2048]{2,1,0:T(8,128)(2,1)} %all-to-all-done, s32[1024]{0:T(1024)S(1)} %pad_clamp_fusion.2), kind=kCustom, calls=%fused_computation.1 | custom fusion | bytes 12583168 | tf_op jit(solution)/shard_map/gather | solution.py:32
  138.2 14.2 %ragged-dot-none.1 = f32[1536,768]{1,0:T(8,128)} custom-call(s32[1]{0:T(128)} %get-tuple-element.41, s32[3]{0:T(128)} %get-tuple-element.42, s32[7]{0:T(128)} %get-tuple-element.43, s32[7]{0:T(128)} %get-tuple-element.44, s32[1]{0:T(128)} %get-tuple-element.41, bf16[1536,2048]{1,0:T(8,128)(2,1)} %bitcast.113, bf16[2,2048,768]{2,1,0:T(8,128)(2,1)} %reshape.140), custom_call_target="tpu_custom_call" | custom-call | flops 4831838208 | bytes 17301512 | tf_op jit(solution)/shard_map/ragged_dot_general/ragged-dot-none
  152.5 4.1 fusion.15
  156.6 12.4 %ragged-dot-none = f32[1536,2048]{1,0:T(8,128)} custom-call(s32[1]{0:T(128)} %get-tuple-element.41, s32[3]{0:T(128)} %get-tuple-element.42, s32[7]{0:T(128)} %get-tuple-element.43, s32[7]{0:T(128)} %get-tuple-element.44, s32[1]{0:T(128)} %get-tuple-element.41, bf16[1536,384]{1,0:T(8,128)(2,1)} %fusion.15, bf16[2,384,2048]{2,1,0:T(8,128)(2,1)} %param.18), custom_call_target="tpu_custom_call" | custom-call | flops 2415919104 | bytes 16908296 | tf_op jit(solution)/shard_map/ragged_dot_general/ragged-dot-none
  169.0 10.4 %gather_fusion.2 = f32[64,24,2048]{2,1,0:T(8,128)} fusion(f32[64,24,2048]{2,1,0:T(8,128)} %bitcast.105, s32[1024]{0:T(1024)S(1)} %pad_clamp_fusion.1), kind=kCustom, calls=%fused_computation.2 | custom fusion | bytes 25166080 | tf_op jit(solution)/shard_map/gather | solution.py:45
  179.4 19.4 %collective-permute-done = f32[64,24,2048]{2,1,0:T(8,128)S(1)} collective-permute-done((f32[64,24,2048]{2,1,0:T(8,128)}, f32[64,24,2048]{2,1,0:T(8,128)S(1)}, u32[]{:S(2)}, u32[]{:S(2)}) %collective-permute-start) | collective-permute-done | bytes 12582944 | tf_op jit(solution)/shard_map/ppermute | solution.py:18
  198.8 8.5 %add_convert_fusion = bf16[64,24,2048]{2,1,0:T(8,128)(2,1)} fusion(f32[64,24,2048]{2,1,0:T(8,128)} %gather_fusion.2, f32[64,24,2048]{2,1,0:T(8,128)S(1)} %collective-permute-done), kind=kLoop, calls=%fused_computation.25 | loop fusion | flops 6291456 | bytes 31457280 | tf_op jit(solution)/shard_map/convert_element_type | solution.py:83
  207.3 7.6 %all-to-all-start.1 = ((bf16[64,24,2048]{2,1,0:T(8,128)(2,1)}), bf16[64,24,2048]{2,1,0:T(8,128)(2,1)}, u32[]{:S(2)}, u32[]{:S(2)}) async-start(bf16[64,24,2048]{2,1,0:T(8,128)(2,1)} %add_convert_fusion), calls=%async_computation.1 | async-start | bytes 12582912 | tf_op jit(solution)/shard_map/all_to_all | solution.py:82
  214.9 10.4 %all-gather.2.cloned.1.call-start = ((), (), s32[]{:S(2)}) async-start(), calls=%async_computation.2 | async-start | bytes 8519680 | tf_op jit(solution)/shard_map/all_gather | solution.py:123
  225.5 2.0 copy.71
  227.5 2.5 copy.62
  230.0 66.1 %all-to-all-done.1 = bf16[64,24,2048]{2,1,0:T(8,128)(2,1)} async-done(((bf16[64,24,2048]{2,1,0:T(8,128)(2,1)}), bf16[64,24,2048]{2,1,0:T(8,128)(2,1)}, u32[]{:S(2)}, u32[]{:S(2)}) %all-to-all-start.1) | async-done | bytes 6291488 | tf_op jit(solution)/shard_map/all_to_all | solution.py:82
  296.2 12.5 %gather_fusion.3 = bf16[1024,2048]{1,0:T(8,128)(2,1)} fusion(bf16[1536,2048]{1,0:T(8,128)(2,1)} %bitcast.10, s32[1024]{0:T(1024)S(1)} %broadcast_clamp_fusion), kind=kCustom, calls=%fused_computation.3 | custom fusion | bytes 8392704 | tf_op jit(solution)/shard_map/gather | solution.py:87
  308.6 6.7 %fusion.14 = f32[128,2048]{1,0:T(8,128)S(1)} fusion(bf16[1024,2048]{1,0:T(8,128)(2,1)} %gather_fusion.3, f32[128,8]{1,0:T(8,128)S(1)} %copy.61), kind=kLoop, calls=%fused_computation.27 | loop fusion | flops 6029312 | bytes 5246976 | tf_op jit(solution)/shard_map/reduce_sum | solution.py:91
  317.3 4.7 fusion.29
  323.6 90.7 %all-gather.2.cloned.1.call-done = bf16[8192,2,256]{0,2,1:T(8,128)(2,1)} async-done(((bf16[128,2,256]{0,2,1:T(8,128)(2,1)}), bf16[8192,2,256]{0,2,1:T(8,128)(2,1)}) %all-gather.2.cloned.1.call-update) | async-done | bytes 8388624 | tf_op jit(solution)/shard_map/all_gather | solution.py:123
  414.2 16.5 %copy.72 = bf16[64,8,8,1024]{3,2,1,0:T(8,128)(2,1)} copy(bf16[64,8,8,1024]{3,1,2,0:T(8,128)(2,1)} %bitcast.110) | data formatting | bytes 16777216
  430.7 12.0 %copy.66 = bf16[8,1024,2,2,128]{4,1,3,2,0:T(8,128)(2,1)} copy(bf16[8,1024,2,2,128]{1,0,4,3,2:T(8,128)(2,1)} %bitcast.106) | data formatting | bytes 16777216
  442.7 111.7 %while.15 = (s32[]{:T(128)}, f32[2,1024]{1,0:T(2,128)S(1)}, f32[2,1024]{1,0:T(2,128)S(1)}, f32[2,1024,128]{2,1,0:T(8,128)S(1)}, bf16[8,1024,2,2,128]{4,1,3,2,0:T...) while((s32[]{:T(128)}, f32[2,1024]{1,0:T(2,128)S(1)}, ...), condition=%wide.region_14.15_spmd.clone, body=%wide.region_11.14_spmd.clone.sunk | while | flops 1091315712 | bytes 64618624 | solution.py:148
  442.7 1.3 dynamic-slice_bitcast_fusion.2
  444.1 4.5 bitcast_reduce_fusion.2
  448.5 4.9 fusion.42
  454.3 2.4 fusion.44
  456.7 1.3 dynamic-slice_bitcast_fusion.2
  458.0 4.5 bitcast_reduce_fusion.2
  462.5 4.9 fusion.42
  468.3 2.4 fusion.44
  470.7 1.3 dynamic-slice_bitcast_fusion.2
  472.0 4.5 bitcast_reduce_fusion.2
  476.5 4.9 fusion.42
  481.4 0.8 copy-done
  482.2 2.4 fusion.44
  484.6 1.3 dynamic-slice_bitcast_fusion.2
  486.0 4.5 bitcast_reduce_fusion.2
  490.4 4.9 fusion.42
  496.2 2.4 fusion.44
  498.6 1.3 dynamic-slice_bitcast_fusion.2
  499.9 4.5 bitcast_reduce_fusion.2
  504.4 4.9 fusion.42
  510.2 2.4 fusion.44
  512.6 1.3 dynamic-slice_bitcast_fusion.2
  513.9 4.5 bitcast_reduce_fusion.2
  518.4 4.9 fusion.42
  523.3 0.8 copy-done
  524.1 2.4 fusion.44
  526.6 1.3 dynamic-slice_bitcast_fusion.2
  527.9 4.5 bitcast_reduce_fusion.2
  532.3 4.9 fusion.42
  538.1 2.4 fusion.44
  540.5 1.3 dynamic-slice_bitcast_fusion.2
  541.8 4.5 bitcast_reduce_fusion.2
  546.3 4.9 fusion.42
  552.1 2.4 fusion.44
  555.2 0.9 copy.78
  (107 shorter events, 13.3 us)
Async XLA Ops:
  40.3 11.9 %copy-start.5 = (s32[8192]{0:T(1024)S(1)}, s32[8192]{0:T(1024)}, u32[]{:S(2)}) copy-start(s32[8192]{0:T(1024)} %param.14) | copy-start | bytes 98308
  40.3 91.6 %all-to-all-start = ((bf16[64,24,2048]{2,1,0:T(8,128)(2,1)}), bf16[64,24,2048]{2,1,0:T(8,128)(2,1)}, u32[]{:S(2)}, u32[]{:S(2)}) async-start(bf16[64,24,2048]{2,1,0:T(8,128)(2,1)} %bitcast.107), calls=%async_computation | async-start | bytes 12582912 | tf_op jit(solution)/shard_map/all_to_all | solution.py:76
  179.4 19.4 %collective-permute-start = (f32[64,24,2048]{2,1,0:T(8,128)}, f32[64,24,2048]{2,1,0:T(8,128)S(1)}, u32[]{:S(2)}, u32[]{:S(2)}) collective-permute-start(f32[64,24,2048]{2,1,0:T(8,128)} %gather_fusion.2), channel_id=1, source_target_pairs={{0,1},{1,0},{2,3},{3,2},{4,5},{5,4},{6,7},{7,6},{8,9},{9,8},{10,11... | collective-permute-start | bytes 37748744 | tf_op jit(solution)/shard_map/ppermute | solution.py:18
  207.3 18.1 %copy-start.6 = (f32[128,8]{0,1:T(8,128)S(1)}, f32[128,8]{0,1:T(8,128)}, u32[]{:S(2)}) copy-start(f32[128,8]{0,1:T(8,128)} %param.16) | copy-start | bytes 12292
  207.3 88.9 %all-to-all-start.1 = ((bf16[64,24,2048]{2,1,0:T(8,128)(2,1)}), bf16[64,24,2048]{2,1,0:T(8,128)(2,1)}, u32[]{:S(2)}, u32[]{:S(2)}) async-start(bf16[64,24,2048]{2,1,0:T(8,128)(2,1)} %add_convert_fusion), calls=%async_computation.1 | async-start | bytes 12582912 | tf_op jit(solution)/shard_map/all_to_all | solution.py:82
  214.9 199.3 %all-gather.2.cloned.1.call-start = ((), (), s32[]{:S(2)}) async-start(), calls=%async_computation.2 | async-start | bytes 8519680 | tf_op jit(solution)/shard_map/all_gather | solution.py:123
  296.2 19.1 %copy-start.3 = (bf16[128,2048]{1,0:T(8,128)(2,1)S(1)}, bf16[128,2048]{1,0:T(8,128)(2,1)}, u32[]{:S(2)}) copy-start(bf16[128,2048]{1,0:T(8,128)(2,1)} %param.13) | copy-start | bytes 1572868
  308.6 6.9 %copy-start.2 = (bf16[512,2048]{1,0:T(8,128)(2,1)S(1)}, bf16[512,2048]{1,0:T(8,128)(2,1)}, u32[]{:S(2)}) copy-start(bf16[512,2048]{1,0:T(8,128)(2,1)} %copy.62) | copy-start | bytes 6291460
  308.6 7.0 %copy-start.4 = (f32[2048]{0:T(1024)S(1)}, f32[2048]{0:T(1024)}, u32[]{:S(2)}) copy-start(f32[2048]{0:T(1024)} %param.19) | copy-start | bytes 24580
  308.6 7.8 %copy-start.8 = (f32[128]{0:T(128)S(1)}, f32[128]{0:T(128)}, u32[]{:S(2)}) copy-start(f32[128]{0:T(128)} %param.23) | copy-start | bytes 1540
  315.6 6.4 %copy-start.1 = (f32[128,2048]{1,0:T(8,128)}, f32[128,2048]{1,0:T(8,128)S(1)}, u32[]{:S(2)}) copy-start(f32[128,2048]{1,0:T(8,128)S(1)} %get-tuple-element.109) | copy-start | bytes 3145732
  322.0 1.1 copy-start.7
  448.5 5.8 %copy-start = (f32[2,1024,1024]{2,1,0:T(8,128)S(1)}, f32[2,1024,1024]{2,1,0:T(8,128)}, u32[]{:S(2)}) copy-start(f32[2,1024,1024]{2,1,0:T(8,128)} %get-tuple-element.154) | copy-start | bytes 25165828 | tf_op jit(solution)/shard_map/while
  462.5 5.8 %copy-start = (f32[2,1024,1024]{2,1,0:T(8,128)S(1)}, f32[2,1024,1024]{2,1,0:T(8,128)}, u32[]{:S(2)}) copy-start(f32[2,1024,1024]{2,1,0:T(8,128)} %get-tuple-element.154) | copy-start | bytes 25165828 | tf_op jit(solution)/shard_map/while
  476.5 5.8 %copy-start = (f32[2,1024,1024]{2,1,0:T(8,128)S(1)}, f32[2,1024,1024]{2,1,0:T(8,128)}, u32[]{:S(2)}) copy-start(f32[2,1024,1024]{2,1,0:T(8,128)} %get-tuple-element.154) | copy-start | bytes 25165828 | tf_op jit(solution)/shard_map/while
  490.4 5.8 %copy-start = (f32[2,1024,1024]{2,1,0:T(8,128)S(1)}, f32[2,1024,1024]{2,1,0:T(8,128)}, u32[]{:S(2)}) copy-start(f32[2,1024,1024]{2,1,0:T(8,128)} %get-tuple-element.154) | copy-start | bytes 25165828 | tf_op jit(solution)/shard_map/while
  504.4 5.8 %copy-start = (f32[2,1024,1024]{2,1,0:T(8,128)S(1)}, f32[2,1024,1024]{2,1,0:T(8,128)}, u32[]{:S(2)}) copy-start(f32[2,1024,1024]{2,1,0:T(8,128)} %get-tuple-element.154) | copy-start | bytes 25165828 | tf_op jit(solution)/shard_map/while
  518.4 5.8 %copy-start = (f32[2,1024,1024]{2,1,0:T(8,128)S(1)}, f32[2,1024,1024]{2,1,0:T(8,128)}, u32[]{:S(2)}) copy-start(f32[2,1024,1024]{2,1,0:T(8,128)} %get-tuple-element.154) | copy-start | bytes 25165828 | tf_op jit(solution)/shard_map/while
  532.3 5.8 %copy-start = (f32[2,1024,1024]{2,1,0:T(8,128)S(1)}, f32[2,1024,1024]{2,1,0:T(8,128)}, u32[]{:S(2)}) copy-start(f32[2,1024,1024]{2,1,0:T(8,128)} %get-tuple-element.154) | copy-start | bytes 25165828 | tf_op jit(solution)/shard_map/while
  546.3 5.8 %copy-start = (f32[2,1024,1024]{2,1,0:T(8,128)S(1)}, f32[2,1024,1024]{2,1,0:T(8,128)}, u32[]{:S(2)}) copy-start(f32[2,1024,1024]{2,1,0:T(8,128)} %get-tuple-element.154) | copy-start | bytes 25165828 | tf_op jit(solution)/shard_map/while
Sparse Core Ops, SparseCore 0:
  317.4 96.8 all-gather.1
where the time goes:
time: 573 us; the launch traced here: 563 us
  waiting for transfers between devices  233 us (41%)
  local copies, waits for them, and re-layouts  110 us (19%)
  other arithmetic  85.3 us (15%)
  matrix products  60.3 us (11%)
  starting transfers between devices  29.9 us (5%)
  Pallas kernels  28 us (5%)
  between operations  16.1 us (3%)
    all_gather x1, waiting for transfers between devices, body(): kv_piece = lax.all_gather(stacked, 'expert', axis=0, tiled=True)  90.7 us
    all_to_all x1, waiting for transfers between devices, body(): lax.all_to_all(combined.astype(jnp.bfloat16), 'expert', split_axis=0, con...  66.1 us
    all_to_all x1, waiting for transfers between devices, body(): lax.all_to_all(outgoing, 'expert', split_axis=0, concat_axis=0, tiled=True)  57 us
    reduce_sum x8, other arithmetic, step_block(): totals_out = totals_in * rescale + jnp.sum(weights, axis=-1)  39.3 us
    dot_general x8, matrix products, step_block(): jnp.einsum('hrd,khd->hrk', grouped_queries, kv_block[:, 0], preferred_ele...  35.7 us
    unnamed x24, local copies, waits for them, and re-layouts  32.8 us
    another operation x2, Pallas kernels  26.6 us
    ppermute x1, waiting for transfers between devices, from_partner(): return lax.ppermute(block, axis, route)  19.4 us
  transfers between devices with their start and end apart: 4, of which 4 were waited for; matrix products, arithmetic and copies ran while one was open for 5% of the time, Pallas kernels for 0%

commit v1 on v0

v1 whole, which is shorter than its diff:
```python
import functools
import jax
import jax.numpy as jnp
from jax import lax
from jax.experimental import pallas as pl
from jax.experimental.pallas import tpu as pltpu
from jax.sharding import PartitionSpec as P

EPSILON = 1e-06
MESH = pl.DeviceIdType.MESH
F32 = jnp.float32
BF16 = jnp.bfloat16

CHIPS = 64
CAP = 24
TOK = 128
D = 2048
HD = 1024
UNITS = 384
PER = 8
BATCHES = CHIPS // PER
ROWS = PER * CAP


def offsets(n):
    a, b, c = n // 16, (n // 4) % 4, n % 4
    return c, (c + b) % 4, (c + a) % 4


def chip_plus(chip, n):
    oy, oz, ox = offsets(n)
    y, z, x = chip // 16, (chip // 4) % 4, chip % 4
    return ((y + oy) % 4) * 16 + ((z + oz) % 4) * 4 + (x + ox) % 4


def chip_minus(chip, n):
    oy, oz, ox = offsets(n)
    y, z, x = chip // 16, (chip // 4) % 4, chip % 4
    return ((y + 4 - oy) % 4) * 16 + ((z + 4 - oz) % 4) * 4 + (x + 4 - ox) % 4


def slot_group(c):
    return (c * 2731) >> 16


def moe_kernel(
    x_ref, mod_ref, ids_ref, rw_ref, wgu_hbm, wd_hbm, gain_ref, wq_hbm, wkv_hbm, qg_ref, kg_ref,
    ho_ref, q_ref, kv_ref,
    wraw, w_s, wd_s, wq_s, kvraw, kvw_s, out_s, a_s, b_s, ret_s, rin_s, gu_s, own_s, ps_s, pr_s,
    mask_s, val_s, hi_s, lo_s, valt_s, acc_s, nrm_s,
    wsem, dsend, drecv, fsend, frecv, psend, precv, rsend, rrecv, hsend, hrecv,
):
    me = lax.axis_index("expert")
    core = lax.axis_index("half")
    mate = 1 - core
    own = pl.multiple_of(core * HD, HD)
    oth = pl.multiple_of(mate * HD, HD)

    loads = [
        pltpu.make_async_copy(wgu_hbm, wraw, wsem.at[0]),
        pltpu.make_async_copy(wd_hbm, wd_s, wsem.at[1]),
        pltpu.make_async_copy(wkv_hbm, kvraw, wsem.at[2]),
        pltpu.make_async_copy(wq_hbm, wq_s, wsem.at[3]),
    ]
    for load in loads:
        load.start()

    barrier = pltpu.get_barrier_semaphore()
    pl.semaphore_signal(barrier, inc=1, device_id={"expert": me, "half": mate}, device_id_type=MESH)

    @pl.loop(1, CHIPS)
    def _(n):
        pl.semaphore_signal(
            barrier, inc=1, device_id={"expert": chip_plus(me, n), "half": core}, device_id_type=MESH
        )

    lane = lax.broadcasted_iota(jnp.int32, (TOK, TOK), 1)
    row = lax.broadcasted_iota(jnp.int32, (TOK, TOK), 0)
    la, lb, lc = lane >> 4, (lane >> 2) & 3, lane & 3
    my_y, my_z, my_x = me // 16, (me // 4) % 4, me % 4
    dst_row = (
        ((my_y + lc) & 3) * 16 + ((my_z + lc + lb) & 3) * 4 + ((my_x + lc + la) & 3)
    )
    dst_row = jnp.where(lane < CHIPS, dst_row, -1)
    ids = ids_ref[...]
    rw = rw_ref[...]
    member = jnp.zeros((TOK, TOK), F32)
    weight = jnp.zeros((TOK, TOK), F32)
    for j in range(ids.shape[1]):
        hit = jnp.broadcast_to(ids[:, j : j + 1], (TOK, TOK)) == dst_row
        member = member + jnp.where(hit, 1.0, 0.0)
        weight = weight + jnp.where(hit, jnp.broadcast_to(rw[:, j : j + 1], (TOK, TOK)), 0.0)
    lower = jnp.where(lane < row, 1.0, 0.0).astype(BF16)
    rank = jnp.dot(lower, member.astype(BF16), preferred_element_type=F32)
    val = jnp.where(member > 0.5, rank, -1.0)
    val_s[...] = val.astype(BF16)
    valt_s[...] = val.T.astype(BF16)
    high = weight.astype(BF16)
    hi_s[...] = high
    lo_s[...] = (weight - high.astype(F32)).astype(BF16)

    pl.semaphore_wait(barrier, CHIPS)

    x_own = x_ref[:, pl.ds(own, HD)]

    @pl.loop(0, BATCHES)
    def _(b):
        c = lax.broadcasted_iota(jnp.int32, (ROWS, TOK), 0) + b * ROWS
        group = slot_group(c)
        spread = jnp.where(group == lax.broadcasted_iota(jnp.int32, (ROWS, TOK), 1), 1.0, 0.0)
        vals = jnp.dot(spread.astype(BF16), valt_s[...], preferred_element_type=F32)
        pick = jnp.where(vals == (c - CAP * group).astype(F32), 1.0, 0.0).astype(BF16)
        rows_out = jnp.dot(pick, x_own, preferred_element_type=F32).astype(BF16)
        out_s[pl.ds(b * PER, PER)] = rows_out.reshape(PER, CAP, HD)

        @pl.loop(0, PER)
        def _(i):
            n = b * PER + i

            @pl.when(n == 0)
            def _():
                pltpu.make_async_copy(out_s.at[0], a_s.at[0], drecv.at[0]).start()

            @pl.when(n > 0)
            def _():
                pltpu.make_async_remote_copy(
                    src_ref=out_s.at[n],
                    dst_ref=a_s.at[n],
                    send_sem=dsend,
                    recv_sem=drecv.at[b],
                    device_id={"expert": chip_plus(me, n), "half": core},
                    device_id_type=MESH,
                ).start()

    @pl.loop(0, CHIPS)
    def _(n):
        mask_s[n] = jnp.full((CAP, 128), mod_ref[chip_minus(me, n), 0], jnp.int32).astype(F32)

    prow = lax.broadcasted_iota(jnp.int32, (256, 256), 0)
    pcol = lax.broadcasted_iota(jnp.int32, (256, 256), 1)
    part = jnp.where(pcol == jnp.where(prow < 128, 2 * prow, 2 * prow - 255), 1.0, 0.0).astype(BF16)
    loads[0].wait()

    @pl.loop(0, D // 128)
    def _(r):
        r0 = pl.multiple_of(r * 128, 128)
        for e in range(2):
            block = wraw[e, pl.ds(r0, 128)].reshape(256, UNITS)
            parted = jnp.dot(part, block, preferred_element_type=F32).astype(BF16)
            w_s[pl.ds(r0, 128), e * 2 * UNITS : e * 2 * UNITS + UNITS] = parted[:128]
            w_s[pl.ds(r0, 128), e * 2 * UNITS + UNITS : (e + 1) * 2 * UNITS] = parted[128:]

    loads[2].wait()

    @pl.loop(0, D // 128)
    def _(r):
        r0 = pl.multiple_of(r * 128, 128)
        block = kvraw[pl.ds(r0, 128)].reshape(256, 256)
        parted = jnp.dot(part, block, preferred_element_type=F32).astype(BF16)
        kvw_s[pl.ds(r0, 128), 0:256] = parted[:128]
        kvw_s[pl.ds(r0, 128), 256:512] = parted[128:]

    loads[1].wait()

    def pieces(ref, b):
        return ref.at[pl.ds(b * PER, PER)]

    def forward(b):
        pltpu.make_async_copy(pieces(a_s, b), pieces(a_s, b), drecv.at[b]).wait()
        pltpu.make_async_remote_copy(
            src_ref=pieces(a_s, b),
            dst_ref=pieces(b_s, b),
            send_sem=fsend.at[b],
            recv_sem=frecv.at[b],
            device_id={"expert": me, "half": mate},
            device_id_type=MESH,
        ).start()

    forward(0)

    @pl.loop(0, BATCHES)
    def _(b):
        pltpu.make_async_remote_copy(
            src_ref=pieces(a_s, b),
            dst_ref=pieces(b_s, b),
            send_sem=fsend.at[b],
            recv_sem=frecv.at[b],
            device_id={"expert": me, "half": mate},
            device_id_type=MESH,
        ).wait()
        xa = a_s[pl.ds(b * PER, PER)].reshape(ROWS, HD)
        xb = b_s[pl.ds(b * PER, PER)].reshape(ROWS, HD)

        @pl.loop(0, 4)
        def _(k):
            cols = pl.ds(pl.multiple_of(k * UNITS, 128), UNITS)
            gu_s[:, cols] = jnp.dot(
                xa, w_s[pl.ds(own, HD), cols], preferred_element_type=F32
            ) + jnp.dot(xb, w_s[pl.ds(oth, HD), cols], preferred_element_type=F32)

        mask = mask_s[pl.ds(b * PER, PER)].reshape(ROWS, 128)
        image = jnp.concatenate([mask, mask, mask], axis=1) > 0.5
        gate = jnp.where(image, gu_s[:, 2 * UNITS : 3 * UNITS], gu_s[:, :UNITS])
        up = jnp.where(image, gu_s[:, 3 * UNITS :], gu_s[:, UNITS : 2 * UNITS])
        act = gate / (1.0 + jnp.exp(-gate)) * up
        both = jnp.concatenate(
            [jnp.where(image, 0.0, act), jnp.where(image, act, 0.0)], axis=1
        ).astype(BF16)

        ps_s[...] = jnp.dot(both, wd_s[:, pl.ds(oth, HD)], preferred_element_type=F32)
        swap = pltpu.make_async_remote_copy(
            src_ref=ps_s,
            dst_ref=pr_s.at[b % 2],
            send_sem=psend,
            recv_sem=precv.at[b % 2],
            device_id={"expert": me, "half": mate},
            device_id_type=MESH,
        )
        swap.start()
        own_s[...] = jnp.dot(both, wd_s[:, pl.ds(own, HD)], preferred_element_type=F32)
        swap.wait()
        ret_s[pl.ds(b * PER, PER)] = (own_s[...] + pr_s[b % 2]).astype(BF16).reshape(PER, CAP, HD)

        @pl.loop(0, PER)
        def _(i):
            n = b * PER + i

            @pl.when(n == 0)
            def _():
                pltpu.make_async_copy(ret_s.at[0], rin_s.at[0], rrecv.at[0]).start()

            @pl.when(n > 0)
            def _():
                pltpu.make_async_remote_copy(
                    src_ref=ret_s.at[n],
                    dst_ref=rin_s.at[n],
                    send_sem=rsend,
                    recv_sem=rrecv.at[b],
                    device_id={"expert": chip_minus(me, n), "half": core},
                    device_id_type=MESH,
                ).start()

        @pl.when(b < BATCHES - 1)
        def _():
            forward(b + 1)

    acc_s[...] = x_ref[:, pl.ds(own, HD)].astype(F32)
    wide = 2 * ROWS

    @pl.loop(0, BATCHES // 2)
    def _(b):
        c = lax.broadcasted_iota(jnp.int32, (TOK, wide), 1) + b * wide
        group = slot_group(c)
        spread = jnp.where(group == lax.broadcasted_iota(jnp.int32, (TOK, wide), 0), 1.0, 0.0).astype(BF16)
        vals = jnp.dot(val_s[...], spread, preferred_element_type=F32)
        pick = vals == (c - CAP * group).astype(F32)
        w_hi = jnp.where(pick, jnp.dot(hi_s[...], spread, preferred_element_type=F32), 0.0).astype(BF16)
        w_lo = jnp.where(pick, jnp.dot(lo_s[...], spread, preferred_element_type=F32), 0.0).astype(BF16)
        for k in range(2):
            pltpu.make_async_copy(pieces(rin_s, 2 * b + k), pieces(rin_s, 2 * b + k), rrecv.at[2 * b + k]).wait()
        back = rin_s[pl.ds(b * 2 * PER, 2 * PER)].reshape(wide, HD)
        acc_s[...] += jnp.dot(w_hi, back, preferred_element_type=F32) + jnp.dot(
            w_lo, back, preferred_element_type=F32
        )

    ho_ref[:, pl.ds(own, HD)] = acc_s[...]
    share = pltpu.make_async_remote_copy(
        src_ref=acc_s,
        dst_ref=ho_ref.at[:, pl.ds(own, HD)],
        send_sem=hsend,
        recv_sem=hrecv,
        device_id={"expert": me, "half": mate},
        device_id_type=MESH,
    )
    share.start()
    loads[3].wait()
    share.wait()
    hidden = ho_ref[...]
    mean_sq = jnp.mean(hidden * hidden, axis=-1, keepdims=True)
    nrm_s[...] = (hidden * lax.rsqrt(mean_sq + EPSILON) * gain_ref[...]).astype(BF16)

    def head_norm(values, gain):
        scale = lax.rsqrt(jnp.mean(values * values, axis=-1, keepdims=True) + EPSILON)
        return (values * scale * gain).astype(BF16)

    @pl.loop(0, 4)
    def _(k):
        kv = jnp.dot(nrm_s[...], kvw_s[:, pl.ds(pl.multiple_of(k * 128, 128), 128)], preferred_element_type=F32)

        @pl.when(k < 2)
        def _():
            kv_ref[k] = head_norm(kv, kg_ref[...])

        @pl.when(k >= 2)
        def _():
            kv_ref[k] = kv.astype(BF16)

    @pl.loop(0, 8)
    def _(k):
        q2 = jnp.dot(nrm_s[...], wq_s[:, pl.ds(pl.multiple_of(k * 256, 256), 256)], preferred_element_type=F32)
        q_ref[2 * k] = head_norm(q2[:, :128], qg_ref[...])
        q_ref[2 * k + 1] = head_norm(q2[:, 128:], qg_ref[...])

    rest = pl.ds(1, CHIPS - 1)
    pltpu.make_async_copy(out_s.at[rest], out_s.at[rest], dsend).wait()
    pltpu.make_async_copy(ret_s.at[rest], ret_s.at[rest], rsend).wait()


def moe_call(x, mod, ids, rw, wgu, wd, gain, wq, wkv, qg, kg):
    vm = pl.BlockSpec(memory_space=pltpu.VMEM)
    hbm = pl.BlockSpec(memory_space=pl.ANY)
    sm = pl.BlockSpec(memory_space=pltpu.SMEM)
    dma = pltpu.SemaphoreType.DMA
    return pl.pallas_call(
        moe_kernel,
        out_shape=(
            jax.ShapeDtypeStruct((TOK, D), F32),
            jax.ShapeDtypeStruct((16, TOK, 128), BF16),
            jax.ShapeDtypeStruct((4, TOK, 128), BF16),
        ),
        in_specs=[vm, sm, vm, vm, hbm, hbm, vm, hbm, hbm, vm, vm],
        out_specs=(vm, vm, vm),
        scratch_shapes=[
            pltpu.VMEM((2, D, 2, UNITS), BF16),
            pltpu.VMEM((D, 4 * UNITS), BF16),
            pltpu.VMEM((2 * UNITS, D), BF16),
            pltpu.VMEM((D, D), BF16),
            pltpu.VMEM((D, 2, 256), BF16),
            pltpu.VMEM((D, 512), BF16),
            pltpu.VMEM((CHIPS, CAP, HD), BF16),
            pltpu.VMEM((CHIPS, CAP, HD), BF16),
            pltpu.VMEM((CHIPS, CAP, HD), BF16),
            pltpu.VMEM((CHIPS, CAP, HD), BF16),
            pltpu.VMEM((CHIPS, CAP, HD), BF16),
            pltpu.VMEM((ROWS, 4 * UNITS), F32),
            pltpu.VMEM((ROWS, HD), F32),
            pltpu.VMEM((ROWS, HD), F32),
            pltpu.VMEM((2, ROWS, HD), F32),
            pltpu.VMEM((CHIPS, CAP, 128), F32),
            pltpu.VMEM((TOK, TOK), BF16),
            pltpu.VMEM((TOK, TOK), BF16),
            pltpu.VMEM((TOK, TOK), BF16),
            pltpu.VMEM((TOK, TOK), BF16),
            pltpu.VMEM((TOK, HD), F32),
            pltpu.VMEM((TOK, D), BF16),
            dma((4,)),
            dma,
            dma((BATCHES,)),
            dma((BATCHES,)),
            dma((BATCHES,)),
            dma,
            dma((2,)),
            dma,
            dma((BATCHES,)),
            dma,
            dma,
        ],
        compiler_params=pltpu.CompilerParams(
            collective_id=0, has_side_effects=True, vmem_limit_bytes=62 * 1024 * 1024
        ),
    )(x, mod, ids, rw, wgu, wd, gain, wq, wkv, qg, kg)


def body(hidden_in, modality, expert_ids, route_weights, w_gate_up, w_down, norm_gain, w_query,
         key_value_weight, q_gain, k_gain):
    hidden_out, queries, kv_block = moe_call(
        hidden_in, modality.reshape(CHIPS, TOK), expert_ids, route_weights, w_gate_up,
        w_down.reshape(2 * UNITS, D), norm_gain.reshape(1, D), w_query, key_value_weight,
        q_gain.reshape(1, 128), k_gain.reshape(1, 128),
    )
    grouped = queries.reshape(2, 8 * TOK, 128)
    gathered = lax.all_gather(kv_block, "expert", axis=1, tiled=True)
    scores = jnp.einsum("hrd,hkd->hrk", grouped, gathered[:2], preferred_element_type=F32) * 128**-0.5
    peak = jnp.max(scores, axis=-1, keepdims=True)
    weights = jnp.exp(scores - peak)
    totals = jnp.sum(weights, axis=-1, keepdims=True)
    mixed = jnp.einsum("hrk,hkd->hrd", weights.astype(BF16), gathered[2:], preferred_element_type=F32) / totals
    attended = mixed.reshape(16, TOK, 128).transpose(1, 0, 2).reshape(TOK, D).astype(BF16)
    return hidden_out, attended


def solution(mesh):
    in_specs = (
        P("expert", None), P(), P("expert", None), P("expert", None),
        P("expert", None, None, "half"), P("expert", "half", None), P(), P(None, "half"),
        P(None, None, "half"), P(), P(),
    )
    out_specs = (P("expert", None), P("expert", "half"))
    return jax.shard_map(body, mesh=mesh, in_specs=in_specs, out_specs=out_specs, check_vma=False)
```

time: 573 us -> 296 us (0.52); the launches traced: 563 us -> 295 us
  waiting for transfers between devices: 233 us -> 82.4 us
  local copies, waits for them, and re-layouts: 110 us -> 4.73 us
  Pallas kernels: 28 us -> 121 us
  other arithmetic: 85.3 us -> 21.3 us
  starting transfers between devices: 29.9 us -> 0.04 us
  matrix products: 60.3 us -> 51.2 us
    all_to_all x2 -> x0, waiting for transfers between devices: 123 us -> none  [the longest x1 66.1 us: body(): lax.all_to_all(combined.astype(jnp.bfloat16), 'expert', split_axis=0, con...]
    pallas_call x0 -> x1, Pallas kernels: none -> 121 us  [moe_call(): pl.pallas_call(moe_kernel, out_shape=(jax.ShapeDtypeStruct((TOK, D), F32)...]
    gather x4 -> x0, local copies, waits for them, and re-layouts: 36.3 us -> none  [the longest x1 12.5 us: body(): returned.reshape(groups * capacity, part_width)[slot_index]]
    unnamed x24 -> x5, local copies, waits for them, and re-layouts: 32.8 us -> 3.8 us
    another operation x2 -> x0, Pallas kernels: 26.6 us -> none
    reduce_sum x14 -> x1, other arithmetic: 47.3 us -> 21.3 us  [body(): totals = jnp.sum(weights, axis=-1, keepdims=True)]
    all_to_all x2 -> x0, starting transfers between devices: 19.5 us -> none  [the longest x1 11.9 us: body(): lax.all_to_all(outgoing, 'expert', split_axis=0, concat_axis=0, tiled=True)]
    another operation x5 -> x0, other arithmetic: 19.5 us -> none
  transfers between devices with their start and end apart: 4 -> 1, of which waited for: 4 -> 1; matrix products, arithmetic and copies ran while one was open for 5% -> 0% of each run, Pallas kernels for 0% -> 0%
where the time goes in v1:
time: 296 us; the launch traced here: 295 us
  Pallas kernels  121 us (41%)
  waiting for transfers between devices  82.4 us (28%)
  matrix products  51.2 us (17%)
  other arithmetic  21.3 us (7%)
  between operations  14 us (5%)
  local copies, waits for them, and re-layouts  4.73 us (2%)
    pallas_call x1, Pallas kernels, moe_call(): pl.pallas_call(moe_kernel, out_shape=(jax.ShapeDtypeStruct((TOK, D), F32)...  121 us
    all_gather x1, waiting for transfers between devices, body(): gathered = lax.all_gather(kv_block, 'expert', axis=1, tiled=True)  82.4 us
    dot_general x1, matrix products, body(): jnp.einsum('hrd,hkd->hrk', grouped, gathered[:2], preferred_element_type=...  26.1 us
    dot_general x1, matrix products, body(): jnp.einsum('hrk,hkd->hrd', weights.astype(BF16), gathered[2:], preferred_...  25 us
    reduce_sum x1, other arithmetic, body(): totals = jnp.sum(weights, axis=-1, keepdims=True)  21.3 us
  transfers between devices with their start and end apart: 1, of which 1 were waited for; matrix products, arithmetic and copies ran while one was open for 0% of the time, Pallas kernels for 0%

profile of v1, /device:TPU:0, one launch (start us, length us, event | category | flops | bytes accessed | tf_op | source)
XLA Modules:
  0.0 294.9 jit_solution(17604838056980735945)
XLA Ops:
  7.2 0.0 all-gather.2.cloned.1.call-start
  7.2 1.4 copy.13.ids_ref
  8.6 1.4 copy.14.rw_ref
  10.0 121.2 %shard_map.122 = (f32[128,2048]{1,0:T(8,128)}, bf16[16,128,128]{2,1,0:T(8,128)(2,1)}, bf16[4,128,128]{2,1,0:T(8,128)(2,1)}) custom-call(bf16[128,2048]{1,0:T(8,128)(2,1)} %x_ref.1, s32[64,128]{1,0:T(8,128)} %bitcast.18, s32[128,8]{1,0:T(8,128)} %copy.13.ids_ref, f32[128,8]{1,0:T(8,128)} %copy.14.rw_ref, bf16[2,2048,2,384]{3,2,1,0:T(2,128)(2,1)} %wgu_hbm.1, ...), custom_call_target="tpu_custom_call" | custom-call | tf_op jit(solution)/shard_map/pallas_call | solution.py:314
  131.2 0.0 all-gather.2.cloned.1.call-update
  131.2 82.4 %all-gather.2.cloned.1.call-done = bf16[4,8192,128]{2,1,0:T(8,128)(2,1)} async-done(((bf16[4,128,128]{2,1,0:T(8,128)(2,1)}), bf16[4,8192,128]{2,1,0:T(8,128)(2,1)}) %all-gather.2.cloned.1.call-update) | async-done | bytes 8388624 | tf_op jit(solution)/shard_map/all_gather | solution.py:372
  213.6 26.1 %multiply_reduce_fusion = (f32[2,1024]{1,0:T(2,128)S(1)}, f32[2,1024,8192]{2,1,0:T(8,128)}) fusion(bf16[2,1024,128]{2,1,0:T(8,128)(2,1)} %bitcast.15, bf16[4,8192,128]{2,1,0:T(8,128)(2,1)} %all-gather.2.cloned.1.call-done), kind=kOutput, calls=%fused_computation.1 | convolution fusion | flops 4328519680 | bytes 71835648 | tf_op jit(solution)/shard_map/hrd,hkd->hrk/dot_general | solution.py:373
  239.7 0.0 copy-start
  239.8 21.3 %fusion = f32[2,1024]{1,0:T(2,128)S(1)} fusion(f32[2,1024,8192]{2,1,0:T(8,128)} %get-tuple-element.9, f32[2,1024]{1,0:T(2,128)S(1)} %get-tuple-element.8), kind=kLoop, calls=%fused_computation.2 | loop fusion | flops 50329600 | bytes 67125248 | tf_op jit(solution)/shard_map/reduce_sum | solution.py:376
  261.1 25.0 %fusion.12 = bf16[2,1024,128]{2,1,0:T(8,128)(2,1)S(1)} fusion(bf16[4,8192,128]{2,1,0:T(8,128)(2,1)} %all-gather.2.cloned.1.call-done, f32[2,1024,8192]{2,1,0:T(8,128)} %get-tuple-element.9, f32[2,1024]{1,0:T(2,128)S(1)} %get-tuple-element.8, f32[2,1024]{1,0:T(2,128)S(1)} %fusion), kind=kOutput, calls=%fused_computation.9 | convolution fusion | flops 4345823232 | bytes 71843840 | tf_op jit(solution)/shard_map/hrk,hkd->hrd/dot_general | solution.py:377
  286.1 0.9 copy.18
  287.1 0.0 copy-done
  287.1 1.0 copy.20
Async XLA Ops:
  7.2 206.5 %all-gather.2.cloned.1.call-start = ((), (), s32[]{:S(2)}) async-start(), calls=%async_computation | async-start | bytes 8519680 | tf_op jit(solution)/shard_map/all_gather | solution.py:372
  239.7 47.3 %copy-start = (f32[128,2048]{1,0:T(8,128)S(1)}, f32[128,2048]{1,0:T(8,128)}, u32[]{:S(2)}) copy-start(f32[128,2048]{1,0:T(8,128)} %get-tuple-element.12) | copy-start | bytes 3145732
Sparse Core Ops, SparseCore 0:
  131.4 82.2 all-gather.1

commit v2 on v1

--- a/solution.py
+++ b/solution.py
@@ -361,6 +361,205 @@
     )(x, mod, ids, rw, wgu, wd, gain, wq, wkv, qg, kg)
 
 
+LOG2E = 1.4426950408889634
+PARTS = (((2, 0, 1), 48, 0), ((0, 1, 2), 40, 48), ((1, 2, 0), 40, 88))
+QCOLS = 512
+KEYS = 2048
+UNITS_KV = 4
+VROWS = 144
+
+
+def group_shift(k):
+    return k + k // 2 - 2 * (k // 3)
+
+
+def attention_kernel(
+    q_ref, kv_ref, o_ref, buf0, buf1, buf2, kun, vun, vt_s, s0, s1, m_s, acc_s, ssem, rsem
+):
+    me = lax.axis_index("expert")
+    core = lax.axis_index("half")
+    place = (me // 16, (me // 4) % 4, me % 4)
+    bufs = (buf0, buf1, buf2)
+
+    def neighbour(axis, step):
+        moved = [(place[i] + (step if i == axis else 0)) % 4 for i in range(3)]
+        return {"expert": moved[0] * 16 + moved[1] * 4 + moved[2], "half": core}
+
+    barrier = pltpu.get_barrier_semaphore()
+    for axis in range(3):
+        for step in (1, 3):
+            pl.semaphore_signal(barrier, inc=1, device_id=neighbour(axis, step), device_id_type=MESH)
+    spots = []
+    for p, (axes, rows, first) in enumerate(PARTS):
+        a, b, c = (place[i] for i in axes)
+        spots.append((a, b, c))
+        for kind in range(4):
+            bufs[p][c, kind, b, a] = kv_ref[kind, first : first + rows, :]
+    m_s[...] = jnp.full_like(m_s, -1e30)
+    acc_s[...] = jnp.zeros_like(acc_s)
+    vt_s[:, 128:, :] = jnp.ones((2, VROWS - 128, KEYS), BF16)
+    pl.semaphore_wait(barrier, 6)
+
+    def send(p, view, phase, step, mark):
+        pltpu.make_async_remote_copy(
+            src_ref=view,
+            dst_ref=view,
+            send_sem=ssem.at[p, phase],
+            recv_sem=rsem.at[p, mark],
+            device_id=neighbour(PARTS[p][0][phase], step),
+            device_id_type=MESH,
+        ).start()
+
+    def landed(p, view, mark):
+        pltpu.make_async_copy(view, view, rsem.at[p, mark]).wait()
+
+    early, late, every = pl.ds(0, 2), pl.ds(2, 2), pl.ds(0, 4)
+
+    def one(p, shift, kinds):
+        a, b, c = spots[p]
+        return bufs[p].at[c, kinds, b, (a + shift) % 4]
+
+    def line(p, shift, kinds):
+        a, b, c = spots[p]
+        return bufs[p].at[c, kinds, (b + shift) % 4]
+
+    def sheet(p, shift, k, kinds):
+        a, b, c = spots[p]
+        return bufs[p].at[(c + shift) % 4, kinds, (b + group_shift(k)) % 4]
+
+    def ring(view, phase, base):
+        for p in range(3):
+            send(p, view(p, 0, every), phase, 1, base)
+            send(p, view(p, 0, every), phase, 3, base + 1)
+
+    def pass_on(view, phase, base):
+        for p in range(3):
+            landed(p, view(p, 3, every), base)
+            landed(p, view(p, 1, every), base + 1)
+            send(p, view(p, 3, early), phase, 1, base + 2)
+            send(p, view(p, 1, late), phase, 3, base + 3)
+
+    def opposite(view, base):
+        for p in range(3):
+            landed(p, view(p, 2, early), base + 2)
+            landed(p, view(p, 2, late), base + 3)
+
+    def group(k):
+        return lambda p, shift, kinds: sheet(p, shift, k, kinds)
+
+    ring(one, 0, 0)
+    pass_on(one, 0, 0)
+    opposite(one, 0)
+    ring(line, 1, 4)
+    ring(group(0), 2, 8)
+    pass_on(line, 1, 4)
+    ring(group(1), 2, 12)
+    ring(group(2), 2, 16)
+    opposite(line, 4)
+    ring(group(3), 2, 20)
+
+    scale = 128**-0.5 * LOG2E
+
+    def scores(h, r):
+        cols = pl.ds(pl.multiple_of(r * QCOLS, QCOLS), QCOLS)
+        return lax.dot_general(kun[h], q_ref[h, cols], (((1,), (1,)), ((), ())), preferred_element_type=F32)
+
+    def absorb(h, s_ref, r):
+        cols = pl.ds(pl.multiple_of(r * QCOLS, QCOLS), QCOLS)
+        s = s_ref[...]
+        m_old = m_s[h, :, cols]
+        m_new = jnp.maximum(m_old, jnp.max(s, axis=0, keepdims=True))
+        m_s[h, :, cols] = m_new
+        probs = jnp.exp2(s * scale - m_new * scale).astype(BF16)
+        fade = jnp.exp2((m_old - m_new) * scale)
+        acc_s[h, :, cols] = acc_s[h, :, cols] * fade + jnp.dot(vt_s[h], probs, preferred_element_type=F32)
+
+    steps = q_ref.shape[1] // QCOLS
+
+    @pl.loop(0, UNITS_KV)
+    def _(u):
+        @pl.when(u == 1)
+        def _():
+            pass_on(group(0), 2, 8)
+            pass_on(group(1), 2, 12)
+
+        @pl.when(u == 2)
+        def _():
+            pass_on(group(2), 2, 16)
+            pass_on(group(3), 2, 20)
+
+        @pl.when(u == 3)
+        def _():
+            for k in range(4):
+                opposite(group(k), 8 + 4 * k)
+
+        mid = (u % 3 + 1) // 2
+        start = 0
+        for p, (axes, rows, first) in enumerate(PARTS):
+            a, b, c = spots[p]
+            for i in range(4):
+                shift_c = (1 - mid) * 2 * (u // 3) + mid * (3 - 2 * (i // 2))
+                k = (1 - mid) * i + mid * (2 * (u - 1) + i % 2)
+                at_c, at_b = (c + shift_c) % 4, (b + group_shift(k)) % 4
+                for h in range(2):
+                    kun[h, start : start + 4 * rows] = bufs[p][at_c, h, at_b].reshape(4 * rows, 128)
+                    vun[h, start : start + 4 * rows] = bufs[p][at_c, 2 + h, at_b].reshape(4 * rows, 128)
+                start += 4 * rows
+        for h in range(2):
+            vt_s[h, :128, :] = vun[h].T
+
+        s0[...] = scores(0, 0)
+
+        @pl.loop(0, steps)
+        def _(r):
+            s1[...] = scores(1, r)
+            absorb(0, s0, r)
+            s0[...] = scores(0, lax.rem(r + 1, steps))
+            absorb(1, s1, r)
+
+    for h in range(2):
+        for j in range(8):
+            cols = slice(j * 128, (j + 1) * 128)
+            head = acc_s[h, :128, cols] / acc_s[h, 128:129, cols]
+            o_ref[:, (h * 8 + j) * 128 : (h * 8 + j + 1) * 128] = head.T.astype(BF16)
+
+    three = pl.ds(0, 3)
+    for p in range(3):
+        a, b, c = spots[p]
+        view = bufs[p].at[c, :, b, three]
+        pltpu.make_async_copy(view, view, ssem.at[p, 0]).wait()
+        view = bufs[p].at[c, :, three]
+        pltpu.make_async_copy(view, view, ssem.at[p, 1]).wait()
+        view = bufs[p].at[three]
+        pltpu.make_async_copy(view, view, ssem.at[p, 2]).wait()
+
+
+def attention_call(queries, kv_block):
+    vm = pl.BlockSpec(memory_space=pltpu.VMEM)
+    dma = pltpu.SemaphoreType.DMA
+    return pl.pallas_call(
+        attention_kernel,
+        out_shape=jax.ShapeDtypeStruct((TOK, D), BF16),
+        in_specs=[vm, vm],
+        out_specs=vm,
+        scratch_shapes=[pltpu.VMEM((4, 4, 4, 4, rows, 128), BF16) for _, rows, _ in PARTS]
+        + [
+            pltpu.VMEM((2, KEYS, 128), BF16),
+            pltpu.VMEM((2, KEYS, 128), BF16),
+            pltpu.VMEM((2, VROWS, KEYS), BF16),
+            pltpu.VMEM((KEYS, QCOLS), F32),
+            pltpu.VMEM((KEYS, QCOLS), F32),
+            pltpu.VMEM((2, 1, 1024), F32),
+            pltpu.VMEM((2, VROWS, 1024), F32),
+            dma((3, 3)),
+            dma((3, 24)),
+        ],
+        compiler_params=pltpu.CompilerParams(
+            collective_id=1, has_side_effects=True, vmem_limit_bytes=48 * 1024 * 1024
+        ),
+    )(queries, kv_block)
+
+
 def body(hidden_in, modality, expert_ids, route_weights, w_gate_up, w_down, norm_gain, w_query,
          key_value_weight, q_gain, k_gain):
     hidden_out, queries, kv_block = moe_call(
@@ -368,14 +567,7 @@
         w_down.reshape(2 * UNITS, D), norm_gain.reshape(1, D), w_query, key_value_weight,
         q_gain.reshape(1, 128), k_gain.reshape(1, 128),
     )
-    grouped = queries.reshape(2, 8 * TOK, 128)
-    gathered = lax.all_gather(kv_block, "expert", axis=1, tiled=True)
-    scores = jnp.einsum("hrd,hkd->hrk", grouped, gathered[:2], preferred_element_type=F32) * 128**-0.5
-    peak = jnp.max(scores, axis=-1, keepdims=True)
-    weights = jnp.exp(scores - peak)
-    totals = jnp.sum(weights, axis=-1, keepdims=True)
-    mixed = jnp.einsum("hrk,hkd->hrd", weights.astype(BF16), gathered[2:], preferred_element_type=F32) / totals
-    attended = mixed.reshape(16, TOK, 128).transpose(1, 0, 2).reshape(TOK, D).astype(BF16)
+    attended = attention_call(queries.reshape(2, 8 * TOK, 128), kv_block)
     return hidden_out, attended
 
 

time: 296 us -> 186 us (0.63)
  waiting for transfers between devices: 82.4 us -> 0 us
  Pallas kernels: 121 us -> 178 us
  matrix products: 51.2 us -> 0 us
  other arithmetic: 21.3 us -> 0 us
  between operations: 14 us -> 0.66 us
  local copies, waits for them, and re-layouts: 4.73 us -> 7.86 us
    all_gather x1 -> x0, waiting for transfers between devices: 82.4 us -> none  [body(): gathered = lax.all_gather(kv_block, 'expert', axis=1, tiled=True)]
    pallas_call x0 -> x1, Pallas kernels: none -> 56.5 us  [attention_call(): pl.pallas_call(attention_kernel, out_shape=jax.ShapeDtypeStruct((TOK, D),...]
    dot_general x2 -> x0, matrix products: 51.2 us -> none  [the longest x1 26.1 us: body(): jnp.einsum('hrd,hkd->hrk', grouped, gathered[:2], preferred_element_type=...]
    reduce_sum x1 -> x0, other arithmetic: 21.3 us -> none  [body(): totals = jnp.sum(weights, axis=-1, keepdims=True)]
    unnamed x5 -> x8, local copies, waits for them, and re-layouts: 3.8 us -> 7.86 us
  transfers between devices with their start and end apart: 1 -> 0, of which waited for: 1 -> 0; matrix products, arithmetic and copies ran while one was open for 0% -> 0% of each run, Pallas kernels for 0% -> 0%
where the time goes in v2:
time: 186 us
  Pallas kernels  178 us (96%)
  local copies, waits for them, and re-layouts  7.86 us (4%)
    pallas_call x1, Pallas kernels, moe_call(): pl.pallas_call(moe_kernel, out_shape=(jax.ShapeDtypeStruct((TOK, D), F32)...  121 us
    pallas_call x1, Pallas kernels, attention_call(): pl.pallas_call(attention_kernel, out_shape=jax.ShapeDtypeStruct((TOK, D),...  56.5 us
    unnamed x8, local copies, waits for them, and re-layouts  7.86 us

profile of v2, /device:TPU:0, one launch (start us, length us, event | category | flops | bytes accessed | tf_op | source)
XLA Modules:
  0.0 186.1 jit_solution(11153059252792228480)
XLA Ops:
  0.6 1.4 copy.13.ids_ref
  2.0 1.4 copy.14.rw_ref
  3.5 121.0 %shard_map.122 = (f32[128,2048]{1,0:T(8,128)}, bf16[16,128,128]{2,1,0:T(8,128)(2,1)}, bf16[4,128,128]{2,1,0:T(8,128)(2,1)}) custom-call(bf16[128,2048]{1,0:T(8,128)(2,1)} %x_ref.1, s32[64,128]{1,0:T(8,128)} %bitcast.8, s32[128,8]{1,0:T(8,128)} %copy.13.ids_ref, f32[128,8]{1,0:T(8,128)} %copy.14.rw_ref, bf16[2,2048,2,384]{3,2,1,0:T(2,128)(2,1)} %wgu_hbm.1, ...), custom_call_target="tpu_custom_call" | custom-call | tf_op jit(solution)/shard_map/pallas_call | solution.py:314
  124.5 0.0 copy-start
  124.5 1.0 copy-done
  125.6 0.0 copy-start.1
  125.6 0.9 copy-done.1
  126.5 56.5 %shard_map.123 = bf16[128,2048]{1,0:T(8,128)(2,1)S(1)} custom-call(bf16[2,1024,128]{2,1,0:T(8,128)(2,1)S(1)} %bitcast.6, bf16[4,128,128]{2,1,0:T(8,128)(2,1)S(1)} %copy-done.1), custom_call_target="tpu_custom_call" | custom-call | tf_op jit(solution)/shard_map/pallas_call | solution.py:540
  183.0 2.3 %copy.17 = f32[128,2048]{1,0:T(8,128)} copy(f32[128,2048]{1,0:T(8,128)} %get-tuple-element.10) | data formatting | bytes 2097152
  185.3 0.8 copy.18
Async XLA Ops:
  124.5 1.0 copy-start
  125.6 0.9 copy-start.1

commit v3 on v2

--- a/solution.py
+++ b/solution.py
@@ -20,6 +20,7 @@
 PER = 8
 BATCHES = CHIPS // PER
 ROWS = PER * CAP
+AHEAD = 4
 
 
 def offsets(n):
@@ -74,45 +75,31 @@
             barrier, inc=1, device_id={"expert": chip_plus(me, n), "half": core}, device_id_type=MESH
         )
 
+    row = lax.broadcasted_iota(jnp.int32, (TOK, TOK), 0)
     lane = lax.broadcasted_iota(jnp.int32, (TOK, TOK), 1)
-    row = lax.broadcasted_iota(jnp.int32, (TOK, TOK), 0)
-    la, lb, lc = lane >> 4, (lane >> 2) & 3, lane & 3
+    ra, rb, rc = row >> 4, (row >> 2) & 3, row & 3
     my_y, my_z, my_x = me // 16, (me // 4) % 4, me % 4
-    dst_row = (
-        ((my_y + lc) & 3) * 16 + ((my_z + lc + lb) & 3) * 4 + ((my_x + lc + la) & 3)
-    )
-    dst_row = jnp.where(lane < CHIPS, dst_row, -1)
-    ids = ids_ref[...]
-    rw = rw_ref[...]
+    target = ((my_y + rc) & 3) * 16 + ((my_z + rc + rb) & 3) * 4 + ((my_x + rc + ra) & 3)
+    target = jnp.where(row < CHIPS, target, -1)
     member = jnp.zeros((TOK, TOK), F32)
     weight = jnp.zeros((TOK, TOK), F32)
-    for j in range(ids.shape[1]):
-        hit = jnp.broadcast_to(ids[:, j : j + 1], (TOK, TOK)) == dst_row
+    for j in range(ids_ref.shape[0]):
+        hit = jnp.broadcast_to(ids_ref[j : j + 1, :], (TOK, TOK)) == target
         member = member + jnp.where(hit, 1.0, 0.0)
-        weight = weight + jnp.where(hit, jnp.broadcast_to(rw[:, j : j + 1], (TOK, TOK)), 0.0)
-    lower = jnp.where(lane < row, 1.0, 0.0).astype(BF16)
-    rank = jnp.dot(lower, member.astype(BF16), preferred_element_type=F32)
+        weight = weight + jnp.where(hit, jnp.broadcast_to(rw_ref[j : j + 1, :], (TOK, TOK)), 0.0)
+    earlier = jnp.where(row < lane, 1.0, 0.0).astype(BF16)
+    rank = jnp.dot(member.astype(BF16), earlier, preferred_element_type=F32)
     val = jnp.where(member > 0.5, rank, -1.0)
-    val_s[...] = val.astype(BF16)
-    valt_s[...] = val.T.astype(BF16)
+    valt_s[...] = val.astype(BF16)
+    val_s[...] = val.T.astype(BF16)
+    weight = weight.T
     high = weight.astype(BF16)
     hi_s[...] = high
     lo_s[...] = (weight - high.astype(F32)).astype(BF16)
 
     pl.semaphore_wait(barrier, CHIPS)
 
-    x_own = x_ref[:, pl.ds(own, HD)]
-
-    @pl.loop(0, BATCHES)
-    def _(b):
-        c = lax.broadcasted_iota(jnp.int32, (ROWS, TOK), 0) + b * ROWS
-        group = slot_group(c)
-        spread = jnp.where(group == lax.broadcasted_iota(jnp.int32, (ROWS, TOK), 1), 1.0, 0.0)
-        vals = jnp.dot(spread.astype(BF16), valt_s[...], preferred_element_type=F32)
-        pick = jnp.where(vals == (c - CAP * group).astype(F32), 1.0, 0.0).astype(BF16)
-        rows_out = jnp.dot(pick, x_own, preferred_element_type=F32).astype(BF16)
-        out_s[pl.ds(b * PER, PER)] = rows_out.reshape(PER, CAP, HD)
-
+    def dispatch(b):
         @pl.loop(0, PER)
         def _(i):
             n = b * PER + i
@@ -131,6 +118,22 @@
                     device_id={"expert": chip_plus(me, n), "half": core},
                     device_id_type=MESH,
                 ).start()
+
+    x_own = x_ref[:, pl.ds(own, HD)]
+
+    @pl.loop(0, BATCHES)
+    def _(b):
+        c = lax.broadcasted_iota(jnp.int32, (ROWS, TOK), 0) + b * ROWS
+        group = slot_group(c)
+        spread = jnp.where(group == lax.broadcasted_iota(jnp.int32, (ROWS, TOK), 1), 1.0, 0.0)
+        vals = jnp.dot(spread.astype(BF16), valt_s[...], preferred_element_type=F32)
+        pick = jnp.where(vals == (c - CAP * group).astype(F32), 1.0, 0.0).astype(BF16)
+        rows_out = jnp.dot(pick, x_own, preferred_element_type=F32).astype(BF16)
+        out_s[pl.ds(b * PER, PER)] = rows_out.reshape(PER, CAP, HD)
+
+        @pl.when(b < AHEAD)
+        def _():
+            dispatch(b)
 
     @pl.loop(0, CHIPS)
     def _(n):
@@ -239,6 +242,10 @@
                     device_id={"expert": chip_minus(me, n), "half": core},
                     device_id_type=MESH,
                 ).start()
+
+        @pl.when(b + AHEAD < BATCHES)
+        def _():
+            dispatch(b + AHEAD)
 
         @pl.when(b < BATCHES - 1)
         def _():
@@ -381,8 +388,14 @@
     place = (me // 16, (me // 4) % 4, me % 4)
     bufs = (buf0, buf1, buf2)
 
+    def along(i, axis):
+        return 1 - ((i + 6 - axis - core) % 3 + 1) // 2
+
+    def coordinate(axis):
+        return sum(place[i] * along(i, axis) for i in range(3))
+
     def neighbour(axis, step):
-        moved = [(place[i] + (step if i == axis else 0)) % 4 for i in range(3)]
+        moved = [(place[i] + step * along(i, axis)) % 4 for i in range(3)]
         return {"expert": moved[0] * 16 + moved[1] * 4 + moved[2], "half": core}
 
     barrier = pltpu.get_barrier_semaphore()
@@ -391,7 +404,7 @@
             pl.semaphore_signal(barrier, inc=1, device_id=neighbour(axis, step), device_id_type=MESH)
     spots = []
     for p, (axes, rows, first) in enumerate(PARTS):
-        a, b, c = (place[i] for i in axes)
+        a, b, c = (coordinate(axis) for axis in axes)
         spots.append((a, b, c))
         for kind in range(4):
             bufs[p][c, kind, b, a] = kv_ref[kind, first : first + rows, :]
@@ -563,7 +576,7 @@
 def body(hidden_in, modality, expert_ids, route_weights, w_gate_up, w_down, norm_gain, w_query,
          key_value_weight, q_gain, k_gain):
     hidden_out, queries, kv_block = moe_call(
-        hidden_in, modality.reshape(CHIPS, TOK), expert_ids, route_weights, w_gate_up,
+        hidden_in, modality.reshape(CHIPS, TOK), expert_ids.T, route_weights.T, w_gate_up,
         w_down.reshape(2 * UNITS, D), norm_gain.reshape(1, D), w_query, key_value_weight,
         q_gain.reshape(1, 128), k_gain.reshape(1, 128),
     )

time: 186 us -> 162 us (0.87)
  Pallas kernels: 178 us -> 156 us
  local copies, waits for them, and re-layouts: 7.86 us -> 5.03 us
    pallas_call x1, Pallas kernels: 121 us -> 100 us  [moe_call(): pl.pallas_call(moe_kernel, out_shape=(jax.ShapeDtypeStruct((TOK, D), F32)...]
    unnamed x8 -> x6, local copies, waits for them, and re-layouts: 7.86 us -> 5.03 us
where the time goes in v3:
time: 162 us; the launch traced here: 161 us
  Pallas kernels  156 us (96%)
  local copies, waits for them, and re-layouts  5.03 us (3%)
    pallas_call x1, Pallas kernels, moe_call(): pl.pallas_call(moe_kernel, out_shape=(jax.ShapeDtypeStruct((TOK, D), F32)...  100 us
    pallas_call x1, Pallas kernels, attention_call(): pl.pallas_call(attention_kernel, out_shape=jax.ShapeDtypeStruct((TOK, D),...  55.4 us
    unnamed x6, local copies, waits for them, and re-layouts  5.03 us

profile of v3, /device:TPU:0, one launch (start us, length us, event | category | flops | bytes accessed | tf_op | source)
XLA Modules:
  0.0 161.3 jit_solution(16403052415131474550)
XLA Ops:
  0.6 100.2 %shard_map.122 = (f32[128,2048]{1,0:T(8,128)}, bf16[16,128,128]{2,1,0:T(8,128)(2,1)}, bf16[4,128,128]{2,1,0:T(8,128)(2,1)}) custom-call(bf16[128,2048]{1,0:T(8,128)(2,1)} %x_ref.1, s32[64,128]{1,0:T(8,128)} %bitcast.10, s32[8,128]{1,0:T(8,128)} %bitcast.12, f32[8,128]{1,0:T(8,128)} %bitcast.13, bf16[2,2048,2,384]{3,2,1,0:T(2,128)(2,1)} %wgu_hbm.1, ...), custom_call_target="tpu_custom_call" | custom-call | tf_op jit(solution)/shard_map/pallas_call | solution.py:321
  100.8 0.0 copy-start
  100.9 1.0 copy-done
  101.9 0.0 copy-start.1
  101.9 0.9 copy-done.1
  102.8 55.4 %shard_map.123 = bf16[128,2048]{1,0:T(8,128)(2,1)S(1)} custom-call(bf16[2,1024,128]{2,1,0:T(8,128)(2,1)S(1)} %bitcast.8, bf16[4,128,128]{2,1,0:T(8,128)(2,1)S(1)} %copy-done.1), custom_call_target="tpu_custom_call" | custom-call | tf_op jit(solution)/shard_map/pallas_call | solution.py:553
  158.2 2.3 %copy.15 = f32[128,2048]{1,0:T(8,128)} copy(f32[128,2048]{1,0:T(8,128)} %get-tuple-element.10) | data formatting | bytes 2097152
  160.5 0.8 copy.16
Async XLA Ops:
  100.8 1.0 copy-start
  101.9 0.9 copy-start.1

commit v4 on v1

v4 whole, which is shorter than its diff:
```python
import functools
import jax
import jax.numpy as jnp
from jax import lax
from jax.experimental import pallas as pl
from jax.experimental.pallas import tpu as pltpu
from jax.sharding import PartitionSpec as P

EPSILON = 1e-06
MESH = pl.DeviceIdType.MESH
F32 = jnp.float32
BF16 = jnp.bfloat16

CHIPS = 64
CAP = 24
TOK = 128
D = 2048
HD = 1024
UNITS = 384
PER = 8
BATCHES = CHIPS // PER
ROWS = PER * CAP
AHEAD = 4


def offsets(n):
    a, b, c = n // 16, (n // 4) % 4, n % 4
    return c, (c + b) % 4, (c + a) % 4


def chip_plus(chip, n):
    oy, oz, ox = offsets(n)
    y, z, x = chip // 16, (chip // 4) % 4, chip % 4
    return ((y + oy) % 4) * 16 + ((z + oz) % 4) * 4 + (x + ox) % 4


def chip_minus(chip, n):
    oy, oz, ox = offsets(n)
    y, z, x = chip // 16, (chip // 4) % 4, chip % 4
    return ((y + 4 - oy) % 4) * 16 + ((z + 4 - oz) % 4) * 4 + (x + 4 - ox) % 4


def slot_group(c):
    return (c * 2731) >> 16


LOG2E = 1.4426950408889634
PARTS = (((2, 0, 1), 48, 0), ((0, 1, 2), 40, 48), ((1, 2, 0), 40, 88))
QCOLS = 512
KEYS = 1024
UNITS_KV = 8
VROWS = 144


def group_shift(k):
    return k + k // 2 - 2 * (k // 3)


def layer_kernel(
    x_ref, mod_ref, ids_ref, rw_ref, wgu_hbm, wd_hbm, gain_ref, wq_hbm, wkv_hbm, qg_ref, kg_ref,
    ho_ref, att_ref,
    kvw_s, out_s, a_s, b_s, ret_s, rin_s, ps_s, pr_s, val_s, hi_s, lo_s, valt_s, acc_s, nrm_s, q_s,
    buf0, buf1, buf2,
    wsem, dsend, drecv, fsend, frecv, psend, precv, rsend, rrecv, hsend, hrecv, ssem, rsem,
):
    me = lax.axis_index("expert")
    core = lax.axis_index("half")
    mate = 1 - core
    own = pl.multiple_of(core * HD, HD)
    oth = pl.multiple_of(mate * HD, HD)
    place = (me // 16, (me // 4) % 4, me % 4)
    bufs = (buf0, buf1, buf2)

    barrier = pltpu.get_barrier_semaphore()
    pl.semaphore_signal(barrier, inc=1, device_id={"expert": me, "half": mate}, device_id_type=MESH)

    @pl.loop(1, CHIPS)
    def _(n):
        pl.semaphore_signal(
            barrier, inc=1, device_id={"expert": chip_plus(me, n), "half": core}, device_id_type=MESH
        )

    row = lax.broadcasted_iota(jnp.int32, (TOK, TOK), 0)
    lane = lax.broadcasted_iota(jnp.int32, (TOK, TOK), 1)
    ra, rb, rc = row >> 4, (row >> 2) & 3, row & 3
    my_y, my_z, my_x = me // 16, (me // 4) % 4, me % 4
    target = ((my_y + rc) & 3) * 16 + ((my_z + rc + rb) & 3) * 4 + ((my_x + rc + ra) & 3)
    target = jnp.where(row < CHIPS, target, -1)
    member = jnp.zeros((TOK, TOK), F32)
    weight = jnp.zeros((TOK, TOK), F32)
    for j in range(ids_ref.shape[0]):
        hit = jnp.broadcast_to(ids_ref[j : j + 1, :], (TOK, TOK)) == target
        member = member + jnp.where(hit, 1.0, 0.0)
        weight = weight + jnp.where(hit, jnp.broadcast_to(rw_ref[j : j + 1, :], (TOK, TOK)), 0.0)
    earlier = jnp.where(row < lane, 1.0, 0.0).astype(BF16)
    rank = jnp.dot(member.astype(BF16), earlier, preferred_element_type=F32)
    val = jnp.where(member > 0.5, rank, -1.0)
    valt_s[...] = val.astype(BF16)
    val_s[...] = val.T.astype(BF16)
    weight = weight.T
    high = weight.astype(BF16)
    hi_s[...] = high
    lo_s[...] = (weight - high.astype(F32)).astype(BF16)

    pl.semaphore_wait(barrier, CHIPS)

    def pieces(ref, b):
        return ref.at[pl.ds(b * PER, PER)]

    def experts(wraw, w_s, wd_s, kvraw, gu_s, own_s, mask_s):
        loads = [
            pltpu.make_async_copy(wgu_hbm, wraw, wsem.at[0]),
            pltpu.make_async_copy(wd_hbm, wd_s, wsem.at[1]),
            pltpu.make_async_copy(wkv_hbm, kvraw, wsem.at[2]),
        ]
        for load in loads:
            load.start()

        def dispatch(b):
            @pl.loop(0, PER)
            def _(i):
                n = b * PER + i

                @pl.when(n == 0)
                def _():
                    pltpu.make_async_copy(out_s.at[0], a_s.at[0], drecv.at[0]).start()

                @pl.when(n > 0)
                def _():
                    pltpu.make_async_remote_copy(
                        src_ref=out_s.at[n],
                        dst_ref=a_s.at[n],
                        send_sem=dsend,
                        recv_sem=drecv.at[b],
                        device_id={"expert": chip_plus(me, n), "half": core},
                        device_id_type=MESH,
                    ).start()

        x_own = x_ref[:, pl.ds(own, HD)]

        @pl.loop(0, BATCHES)
        def _(b):
            c = lax.broadcasted_iota(jnp.int32, (ROWS, TOK), 0) + b * ROWS
            group = slot_group(c)
            spread = jnp.where(group == lax.broadcasted_iota(jnp.int32, (ROWS, TOK), 1), 1.0, 0.0)
            vals = jnp.dot(spread.astype(BF16), valt_s[...], preferred_element_type=F32)
            pick = jnp.where(vals == (c - CAP * group).astype(F32), 1.0, 0.0).astype(BF16)
            rows_out = jnp.dot(pick, x_own, preferred_element_type=F32).astype(BF16)
            out_s[pl.ds(b * PER, PER)] = rows_out.reshape(PER, CAP, HD)

            @pl.when(b < AHEAD)
            def _():
                dispatch(b)

        @pl.loop(0, CHIPS)
        def _(n):
            mask_s[n] = jnp.full((CAP, 128), mod_ref[chip_minus(me, n), 0], jnp.int32).astype(F32)

        prow = lax.broadcasted_iota(jnp.int32, (256, 256), 0)
        pcol = lax.broadcasted_iota(jnp.int32, (256, 256), 1)
        part = jnp.where(pcol == jnp.where(prow < 128, 2 * prow, 2 * prow - 255), 1.0, 0.0).astype(BF16)
        loads[0].wait()

        @pl.loop(0, D // 128)
        def _(r):
            r0 = pl.multiple_of(r * 128, 128)
            for e in range(2):
                block = wraw[e, pl.ds(r0, 128)].reshape(256, UNITS)
                parted = jnp.dot(part, block, preferred_element_type=F32).astype(BF16)
                w_s[pl.ds(r0, 128), e * 2 * UNITS : e * 2 * UNITS + UNITS] = parted[:128]
                w_s[pl.ds(r0, 128), e * 2 * UNITS + UNITS : (e + 1) * 2 * UNITS] = parted[128:]

        loads[2].wait()

        @pl.loop(0, D // 128)
        def _(r):
            r0 = pl.multiple_of(r * 128, 128)
            block = kvraw[pl.ds(r0, 128)].reshape(256, 256)
            parted = jnp.dot(part, block, preferred_element_type=F32).astype(BF16)
            kvw_s[pl.ds(r0, 128), 0:256] = parted[:128]
            kvw_s[pl.ds(r0, 128), 256:512] = parted[128:]

        loads[1].wait()

        def forward(b):
            pltpu.make_async_copy(pieces(a_s, b), pieces(a_s, b), drecv.at[b]).wait()
            pltpu.make_async_remote_copy(
                src_ref=pieces(a_s, b),
                dst_ref=pieces(b_s, b),
                send_sem=fsend.at[b],
                recv_sem=frecv.at[b],
                device_id={"expert": me, "half": mate},
                device_id_type=MESH,
            ).start()

        forward(0)

        @pl.loop(0, BATCHES)
        def _(b):
            pltpu.make_async_remote_copy(
                src_ref=pieces(a_s, b),
                dst_ref=pieces(b_s, b),
                send_sem=fsend.at[b],
                recv_sem=frecv.at[b],
                device_id={"expert": me, "half": mate},
                device_id_type=MESH,
            ).wait()
            xa = a_s[pl.ds(b * PER, PER)].reshape(ROWS, HD)
            xb = b_s[pl.ds(b * PER, PER)].reshape(ROWS, HD)

            @pl.loop(0, 4)
            def _(k):
                cols = pl.ds(pl.multiple_of(k * UNITS, 128), UNITS)
                gu_s[:, cols] = jnp.dot(
                    xa, w_s[pl.ds(own, HD), cols], preferred_element_type=F32
                ) + jnp.dot(xb, w_s[pl.ds(oth, HD), cols], preferred_element_type=F32)

            mask = mask_s[pl.ds(b * PER, PER)].reshape(ROWS, 128)
            image = jnp.concatenate([mask, mask, mask], axis=1) > 0.5
            gate = jnp.where(image, gu_s[:, 2 * UNITS : 3 * UNITS], gu_s[:, :UNITS])
            up = jnp.where(image, gu_s[:, 3 * UNITS :], gu_s[:, UNITS : 2 * UNITS])
            act = gate / (1.0 + jnp.exp(-gate)) * up
            both = jnp.concatenate(
                [jnp.where(image, 0.0, act), jnp.where(image, act, 0.0)], axis=1
            ).astype(BF16)

            ps_s[...] = jnp.dot(both, wd_s[:, pl.ds(oth, HD)], preferred_element_type=F32)
            swap = pltpu.make_async_remote_copy(
                src_ref=ps_s,
                dst_ref=pr_s.at[b % 2],
                send_sem=psend,
                recv_sem=precv.at[b % 2],
                device_id={"expert": me, "half": mate},
                device_id_type=MESH,
            )
            swap.start()
            own_s[...] = jnp.dot(both, wd_s[:, pl.ds(own, HD)], preferred_element_type=F32)
            swap.wait()
            ret_s[pl.ds(b * PER, PER)] = (own_s[...] + pr_s[b % 2]).astype(BF16).reshape(PER, CAP, HD)

            @pl.loop(0, PER)
            def _(i):
                n = b * PER + i

                @pl.when(n == 0)
                def _():
                    pltpu.make_async_copy(ret_s.at[0], rin_s.at[0], rrecv.at[0]).start()

                @pl.when(n > 0)
                def _():
                    pltpu.make_async_remote_copy(
                        src_ref=ret_s.at[n],
                        dst_ref=rin_s.at[n],
                        send_sem=rsend,
                        recv_sem=rrecv.at[b],
                        device_id={"expert": chip_minus(me, n), "half": core},
                        device_id_type=MESH,
                    ).start()

            @pl.when(b + AHEAD < BATCHES)
            def _():
                dispatch(b + AHEAD)

            @pl.when(b < BATCHES - 1)
            def _():
                forward(b + 1)


    pl.run_scoped(
        experts,
        pltpu.VMEM((2, D, 2, UNITS), BF16),
        pltpu.VMEM((D, 4 * UNITS), BF16),
        pltpu.VMEM((2 * UNITS, D), BF16),
        pltpu.VMEM((D, 2, 256), BF16),
        pltpu.VMEM((ROWS, 4 * UNITS), F32),
        pltpu.VMEM((ROWS, HD), F32),
        pltpu.VMEM((CHIPS, CAP, 128), F32),
    )

    def along(i, axis):
        return 1 - ((i + 6 - axis - core) % 3 + 1) // 2

    def coordinate(axis):
        return sum(place[i] * along(i, axis) for i in range(3))

    def neighbour(axis, step):
        moved = [(place[i] + step * along(i, axis)) % 4 for i in range(3)]
        return {"expert": moved[0] * 16 + moved[1] * 4 + moved[2], "half": core}

    def send(p, view, phase, step, mark):
        pltpu.make_async_remote_copy(
            src_ref=view,
            dst_ref=view,
            send_sem=ssem.at[p, phase],
            recv_sem=rsem.at[p, mark],
            device_id=neighbour(PARTS[p][0][phase], step),
            device_id_type=MESH,
        ).start()

    def landed(p, view, mark):
        pltpu.make_async_copy(view, view, rsem.at[p, mark]).wait()

    early, late, every = pl.ds(0, 2), pl.ds(2, 2), pl.ds(0, 4)

    def one(p, shift, kinds):
        a, b, c = spots[p]
        return bufs[p].at[c, kinds, b, (a + shift) % 4]

    def line(p, shift, kinds):
        a, b, c = spots[p]
        return bufs[p].at[c, kinds, (b + shift) % 4]

    def sheet(p, shift, k, kinds):
        a, b, c = spots[p]
        return bufs[p].at[(c + shift) % 4, kinds, (b + group_shift(k)) % 4]

    def ring(view, phase, base):
        for p in range(3):
            send(p, view(p, 0, every), phase, 1, base)
            send(p, view(p, 0, every), phase, 3, base + 1)

    def pass_on(view, phase, base):
        for p in range(3):
            landed(p, view(p, 3, every), base)
            landed(p, view(p, 1, every), base + 1)
            send(p, view(p, 3, early), phase, 1, base + 2)
            send(p, view(p, 1, late), phase, 3, base + 3)

    def opposite(view, base):
        for p in range(3):
            landed(p, view(p, 2, early), base + 2)
            landed(p, view(p, 2, late), base + 3)

    def group(k):
        return lambda p, shift, kinds: sheet(p, shift, k, kinds)

    spots = [tuple(coordinate(axis) for axis in axes) for axes, _, _ in PARTS]

    def head_norm(values, gain):
        scale = lax.rsqrt(jnp.mean(values * values, axis=-1, keepdims=True) + EPSILON)
        return (values * scale * gain).astype(BF16)

    def project(wq_s):
        load = pltpu.make_async_copy(wq_hbm, wq_s, wsem.at[0])
        load.start()
        acc_s[...] = x_ref[:, pl.ds(own, HD)].astype(F32)
        wide = 2 * ROWS

        @pl.loop(0, BATCHES // 2)
        def _(b):
            c = lax.broadcasted_iota(jnp.int32, (TOK, wide), 1) + b * wide
            group = slot_group(c)
            spread = jnp.where(group == lax.broadcasted_iota(jnp.int32, (TOK, wide), 0), 1.0, 0.0).astype(BF16)
            vals = jnp.dot(val_s[...], spread, preferred_element_type=F32)
            pick = vals == (c - CAP * group).astype(F32)
            w_hi = jnp.where(pick, jnp.dot(hi_s[...], spread, preferred_element_type=F32), 0.0).astype(BF16)
            w_lo = jnp.where(pick, jnp.dot(lo_s[...], spread, preferred_element_type=F32), 0.0).astype(BF16)
            for k in range(2):
                pltpu.make_async_copy(pieces(rin_s, 2 * b + k), pieces(rin_s, 2 * b + k), rrecv.at[2 * b + k]).wait()
            back = rin_s[pl.ds(b * 2 * PER, 2 * PER)].reshape(wide, HD)
            acc_s[...] += jnp.dot(w_hi, back, preferred_element_type=F32) + jnp.dot(
                w_lo, back, preferred_element_type=F32
            )

        ho_ref[:, pl.ds(own, HD)] = acc_s[...]
        share = pltpu.make_async_remote_copy(
            src_ref=acc_s,
            dst_ref=ho_ref.at[:, pl.ds(own, HD)],
            send_sem=hsend,
            recv_sem=hrecv,
            device_id={"expert": me, "half": mate},
            device_id_type=MESH,
        )
        share.start()
        share.wait()
        hidden = ho_ref[...]
        mean_sq = jnp.mean(hidden * hidden, axis=-1, keepdims=True)
        nrm_s[...] = (hidden * lax.rsqrt(mean_sq + EPSILON) * gain_ref[...]).astype(BF16)


        for group_of in range(2):
            pair = jnp.dot(
                nrm_s[...], kvw_s[:, group_of * 256 : (group_of + 1) * 256], preferred_element_type=F32
            )
            for i in range(2):
                rows_kv = pair[:, i * 128 : (i + 1) * 128]
                rows_kv = head_norm(rows_kv, kg_ref[...]) if group_of == 0 else rows_kv.astype(BF16)
                for p, (_, rows, first) in enumerate(PARTS):
                    a, b, c = spots[p]
                    bufs[p][c, 2 * group_of + i, b, a] = rows_kv[first : first + rows]
        ring(one, 0, 0)
        load.wait()

        def queries(first, last):
            @pl.loop(first, last)
            def _(k):
                cols = pl.ds(pl.multiple_of(k * 256, 256), 256)
                q2 = jnp.dot(nrm_s[...], wq_s[:, cols], preferred_element_type=F32)
                for i in range(2):
                    rows_q = pl.ds(pl.multiple_of((2 * (k % 4) + i) * 128, 128), 128)
                    q_s[k // 4, rows_q] = head_norm(q2[:, i * 128 : (i + 1) * 128], qg_ref[...])

        queries(0, 3)
        pass_on(one, 0, 0)
        queries(3, 5)
        opposite(one, 0)
        ring(line, 1, 4)
        ring(group(0), 2, 8)
        queries(5, 8)

    pl.run_scoped(project, pltpu.VMEM((D, D), BF16))

    pass_on(line, 1, 4)
    ring(group(1), 2, 12)
    ring(group(2), 2, 16)

    def attend(kun, vun, vt_s, s0, s1, m_s, sum_s):
        m_s[...] = jnp.full_like(m_s, -1e30)
        sum_s[...] = jnp.zeros_like(sum_s)
        vt_s[:, 128:, :] = jnp.ones((2, VROWS - 128, KEYS), BF16)
        scale = 128**-0.5 * LOG2E

        def scores(h, r):
            cols = pl.ds(pl.multiple_of(r * QCOLS, QCOLS), QCOLS)
            return lax.dot_general(kun[h], q_s[h, cols], (((1,), (1,)), ((), ())), preferred_element_type=F32)

        def absorb(h, s_ref, r):
            cols = pl.ds(pl.multiple_of(r * QCOLS, QCOLS), QCOLS)
            s = s_ref[...]
            m_old = m_s[h, :, cols]
            m_new = jnp.maximum(m_old, jnp.max(s, axis=0, keepdims=True))
            m_s[h, :, cols] = m_new
            probs = jnp.exp2(s * scale - m_new * scale).astype(BF16)
            fade = jnp.exp2((m_old - m_new) * scale)
            sum_s[h, :, cols] = sum_s[h, :, cols] * fade + jnp.dot(vt_s[h], probs, preferred_element_type=F32)

        steps = q_s.shape[1] // QCOLS

        @pl.loop(0, UNITS_KV)
        def _(u):
            @pl.when(u == 1)
            def _():
                opposite(line, 4)
                ring(group(3), 2, 20)

            for k in range(4):

                @pl.when(u == 2 + k)
                def _(k=k):
                    pass_on(group(k), 2, 8 + 4 * k)

            for k in range(2):

                @pl.when(u == 6 + k)
                def _(k=k):
                    opposite(group(2 * k), 8 + 8 * k)
                    opposite(group(2 * k + 1), 12 + 8 * k)

            stage = u // 2
            mid = (stage % 3 + 1) // 2
            start = 0
            for p, (axes, rows, first) in enumerate(PARTS):
                a, b, c = spots[p]
                for i in range(2):
                    shift_c = (1 - mid) * 2 * (stage // 3) + mid * (3 - 2 * i)
                    k = (1 - mid) * (2 * (u % 2) + i) + mid * (u - 2)
                    at_c, at_b = (c + shift_c) % 4, (b + group_shift(k)) % 4
                    for h in range(2):
                        kun[h, start : start + 4 * rows] = bufs[p][at_c, h, at_b].reshape(4 * rows, 128)
                        vun[h, start : start + 4 * rows] = bufs[p][at_c, 2 + h, at_b].reshape(4 * rows, 128)
                    start += 4 * rows
            for h in range(2):
                vt_s[h, :128, :] = vun[h].T

            s0[...] = scores(0, 0)

            @pl.loop(0, steps)
            def _(r):
                s1[...] = scores(1, r)
                absorb(0, s0, r)
                s0[...] = scores(0, lax.rem(r + 1, steps))
                absorb(1, s1, r)

        for h in range(2):
            for j in range(8):
                cols = slice(j * 128, (j + 1) * 128)
                head = sum_s[h, :128, cols] / sum_s[h, 128:129, cols]
                att_ref[:, (h * 8 + j) * 128 : (h * 8 + j + 1) * 128] = head.T.astype(BF16)


    pl.run_scoped(
        attend,
        pltpu.VMEM((2, KEYS, 128), BF16),
        pltpu.VMEM((2, KEYS, 128), BF16),
        pltpu.VMEM((2, VROWS, KEYS), BF16),
        pltpu.VMEM((KEYS, QCOLS), F32),
        pltpu.VMEM((KEYS, QCOLS), F32),
        pltpu.VMEM((2, 1, 1024), F32),
        pltpu.VMEM((2, VROWS, 1024), F32),
    )

    three = pl.ds(0, 3)
    for p in range(3):
        a, b, c = spots[p]
        view = bufs[p].at[c, :, b, three]
        pltpu.make_async_copy(view, view, ssem.at[p, 0]).wait()
        view = bufs[p].at[c, :, three]
        pltpu.make_async_copy(view, view, ssem.at[p, 1]).wait()
        view = bufs[p].at[three]
        pltpu.make_async_copy(view, view, ssem.at[p, 2]).wait()
    rest = pl.ds(1, CHIPS - 1)
    pltpu.make_async_copy(out_s.at[rest], out_s.at[rest], dsend).wait()
    pltpu.make_async_copy(ret_s.at[rest], ret_s.at[rest], rsend).wait()


def layer_call(x, mod, ids, rw, wgu, wd, gain, wq, wkv, qg, kg):
    vm = pl.BlockSpec(memory_space=pltpu.VMEM)
    hbm = pl.BlockSpec(memory_space=pl.ANY)
    sm = pl.BlockSpec(memory_space=pltpu.SMEM)
    dma = pltpu.SemaphoreType.DMA
    return pl.pallas_call(
        layer_kernel,
        out_shape=(jax.ShapeDtypeStruct((TOK, D), F32), jax.ShapeDtypeStruct((TOK, D), BF16)),
        in_specs=[vm, sm, vm, vm, hbm, hbm, vm, hbm, hbm, vm, vm],
        out_specs=(vm, vm),
        scratch_shapes=[
            pltpu.VMEM((D, 512), BF16),
            pltpu.VMEM((CHIPS, CAP, HD), BF16),
            pltpu.VMEM((CHIPS, CAP, HD), BF16),
            pltpu.VMEM((CHIPS, CAP, HD), BF16),
            pltpu.VMEM((CHIPS, CAP, HD), BF16),
            pltpu.VMEM((CHIPS, CAP, HD), BF16),
            pltpu.VMEM((ROWS, HD), F32),
            pltpu.VMEM((2, ROWS, HD), F32),
            pltpu.VMEM((TOK, TOK), BF16),
            pltpu.VMEM((TOK, TOK), BF16),
            pltpu.VMEM((TOK, TOK), BF16),
            pltpu.VMEM((TOK, TOK), BF16),
            pltpu.VMEM((TOK, HD), F32),
            pltpu.VMEM((TOK, D), BF16),
            pltpu.VMEM((2, 8 * TOK, 128), BF16),
        ]
        + [pltpu.VMEM((4, 4, 4, 4, rows, 128), BF16) for _, rows, _ in PARTS]
        + [
            dma((3,)),
            dma,
            dma((BATCHES,)),
            dma((BATCHES,)),
            dma((BATCHES,)),
            dma,
            dma((2,)),
            dma,
            dma((BATCHES,)),
            dma,
            dma,
            dma((3, 3)),
            dma((3, 24)),
        ],
        compiler_params=pltpu.CompilerParams(
            collective_id=0, has_side_effects=True, vmem_limit_bytes=62 * 1024 * 1024
        ),
    )(x, mod, ids, rw, wgu, wd, gain, wq, wkv, qg, kg)


def body(hidden_in, modality, expert_ids, route_weights, w_gate_up, w_down, norm_gain, w_query,
         key_value_weight, q_gain, k_gain):
    return layer_call(
        hidden_in, modality.reshape(CHIPS, TOK), expert_ids.T, route_weights.T, w_gate_up,
        w_down.reshape(2 * UNITS, D), norm_gain.reshape(1, D), w_query, key_value_weight,
        q_gain.reshape(1, 128), k_gain.reshape(1, 128),
    )


def solution(mesh):
    in_specs = (
        P("expert", None), P(), P("expert", None), P("expert", None),
        P("expert", None, None, "half"), P("expert", "half", None), P(), P(None, "half"),
        P(None, None, "half"), P(), P(),
    )
    out_specs = (P("expert", None), P("expert", "half"))
    return jax.shard_map(body, mesh=mesh, in_specs=in_specs, out_specs=out_specs, check_vma=False)
```

time: 296 us -> 155 us (0.52)
  waiting for transfers between devices: 82.4 us -> 0 us
  matrix products: 51.2 us -> 0 us
  Pallas kernels: 121 us -> 150 us
  other arithmetic: 21.3 us -> 0 us
  between operations: 14 us -> 0.64 us
    all_gather x1 -> x0, waiting for transfers between devices: 82.4 us -> none  [body(): gathered = lax.all_gather(kv_block, 'expert', axis=1, tiled=True)]
    dot_general x2 -> x0, matrix products: 51.2 us -> none  [the longest x1 26.1 us: body(): jnp.einsum('hrd,hkd->hrk', grouped, gathered[:2], preferred_element_type=...]
    pallas_call x1, Pallas kernels: 121 us -> 150 us  [layer_call(): pl.pallas_call(layer_kernel, out_shape=(jax.ShapeDtypeStruct((TOK, D), F3...]
    reduce_sum x1 -> x0, other arithmetic: 21.3 us -> none  [body(): totals = jnp.sum(weights, axis=-1, keepdims=True)]
  transfers between devices with their start and end apart: 1 -> 0, of which waited for: 1 -> 0; matrix products, arithmetic and copies ran while one was open for 0% -> 0% of each run, Pallas kernels for 0% -> 0%
where the time goes in v4:
time: 155 us
  Pallas kernels  150 us (97%)
  local copies, waits for them, and re-layouts  4.18 us (3%)
    pallas_call x1, Pallas kernels, layer_call(): pl.pallas_call(layer_kernel, out_shape=(jax.ShapeDtypeStruct((TOK, D), F3...  150 us
    unnamed x2, local copies, waits for them, and re-layouts  4.18 us

profile of v4, /device:TPU:0, one launch (start us, length us, event | category | flops | bytes accessed | tf_op | source)
XLA Modules:
  0.0 155.2 jit_solution(2136916346808480383)
XLA Ops:
  0.6 150.4 %shard_map.122 = (f32[128,2048]{1,0:T(8,128)}, bf16[128,2048]{1,0:T(8,128)(2,1)}) custom-call(bf16[128,2048]{1,0:T(8,128)(2,1)} %x_ref.1, s32[64,128]{1,0:T(8,128)} %bitcast.8, s32[8,128]{1,0:T(8,128)} %bitcast.10, f32[8,128]{1,0:T(8,128)} %bitcast.11, bf16[2,2048,2,384]{3,2,1,0:T(2,128)(2,1)} %wgu_hbm.1, bf16[768,2048]{1,0:T(8,128)(2,1)} %bitcast.7, ...), custom_call_target="tpu_custom_call" | custom-call | tf_op jit(solution)/shard_map/pallas_call | solution.py:521
  151.0 2.3 %copy.15 = f32[128,2048]{1,0:T(8,128)} copy(f32[128,2048]{1,0:T(8,128)} %get-tuple-element.4) | data formatting | bytes 2097152
  153.3 1.9 %copy.16 = bf16[128,2048]{1,0:T(8,128)(2,1)} copy(bf16[128,2048]{1,0:T(8,128)(2,1)} %get-tuple-element.5) | data formatting | bytes 1048576

commit v5 on v4

--- a/solution.py
+++ b/solution.py
@@ -193,78 +193,86 @@
                 device_id_type=MESH,
             ).start()
 
-        forward(0)
-
-        @pl.loop(0, BATCHES)
-        def _(b):
-            pltpu.make_async_remote_copy(
-                src_ref=pieces(a_s, b),
-                dst_ref=pieces(b_s, b),
-                send_sem=fsend.at[b],
-                recv_sem=frecv.at[b],
-                device_id={"expert": me, "half": mate},
-                device_id_type=MESH,
-            ).wait()
-            xa = a_s[pl.ds(b * PER, PER)].reshape(ROWS, HD)
-            xb = b_s[pl.ds(b * PER, PER)].reshape(ROWS, HD)
-
-            @pl.loop(0, 4)
-            def _(k):
-                cols = pl.ds(pl.multiple_of(k * UNITS, 128), UNITS)
-                gu_s[:, cols] = jnp.dot(
-                    xa, w_s[pl.ds(own, HD), cols], preferred_element_type=F32
-                ) + jnp.dot(xb, w_s[pl.ds(oth, HD), cols], preferred_element_type=F32)
-
-            mask = mask_s[pl.ds(b * PER, PER)].reshape(ROWS, 128)
-            image = jnp.concatenate([mask, mask, mask], axis=1) > 0.5
-            gate = jnp.where(image, gu_s[:, 2 * UNITS : 3 * UNITS], gu_s[:, :UNITS])
-            up = jnp.where(image, gu_s[:, 3 * UNITS :], gu_s[:, UNITS : 2 * UNITS])
-            act = gate / (1.0 + jnp.exp(-gate)) * up
-            both = jnp.concatenate(
-                [jnp.where(image, 0.0, act), jnp.where(image, act, 0.0)], axis=1
-            ).astype(BF16)
-
-            ps_s[...] = jnp.dot(both, wd_s[:, pl.ds(oth, HD)], preferred_element_type=F32)
-            swap = pltpu.make_async_remote_copy(
-                src_ref=ps_s,
-                dst_ref=pr_s.at[b % 2],
-                send_sem=psend,
-                recv_sem=precv.at[b % 2],
+        def swap(b):
+            return pltpu.make_async_remote_copy(
+                src_ref=ps_s.at[b % 2],
+                dst_ref=pr_s.at[b % 3],
+                send_sem=psend.at[b % 2],
+                recv_sem=precv.at[b % 3],
                 device_id={"expert": me, "half": mate},
                 device_id_type=MESH,
             )
-            swap.start()
-            own_s[...] = jnp.dot(both, wd_s[:, pl.ds(own, HD)], preferred_element_type=F32)
-            swap.wait()
-            ret_s[pl.ds(b * PER, PER)] = (own_s[...] + pr_s[b % 2]).astype(BF16).reshape(PER, CAP, HD)
-
-            @pl.loop(0, PER)
-            def _(i):
-                n = b * PER + i
-
-                @pl.when(n == 0)
-                def _():
-                    pltpu.make_async_copy(ret_s.at[0], rin_s.at[0], rrecv.at[0]).start()
-
-                @pl.when(n > 0)
-                def _():
-                    pltpu.make_async_remote_copy(
-                        src_ref=ret_s.at[n],
-                        dst_ref=rin_s.at[n],
-                        send_sem=rsend,
-                        recv_sem=rrecv.at[b],
-                        device_id={"expert": chip_minus(me, n), "half": core},
-                        device_id_type=MESH,
-                    ).start()
+
+        forward(0)
+
+        @pl.loop(0, BATCHES + 1)
+        def _(b):
+            @pl.when(b < BATCHES - 1)
+            def _():
+                forward(b + 1)
+
+            @pl.when(b < BATCHES)
+            def _():
+                pltpu.make_async_remote_copy(
+                    src_ref=pieces(a_s, b),
+                    dst_ref=pieces(b_s, b),
+                    send_sem=fsend.at[b],
+                    recv_sem=frecv.at[b],
+                    device_id={"expert": me, "half": mate},
+                    device_id_type=MESH,
+                ).wait()
+                xa = a_s[pl.ds(b * PER, PER)].reshape(ROWS, HD)
+                xb = b_s[pl.ds(b * PER, PER)].reshape(ROWS, HD)
+
+                @pl.loop(0, 4)
+                def _(k):
+                    cols = pl.ds(pl.multiple_of(k * UNITS, 128), UNITS)
+                    gu_s[:, cols] = jnp.dot(
+                        xa, w_s[pl.ds(own, HD), cols], preferred_element_type=F32
+                    ) + jnp.dot(xb, w_s[pl.ds(oth, HD), cols], preferred_element_type=F32)
+
+                mask = mask_s[pl.ds(b * PER, PER)].reshape(ROWS, 128)
+                image = jnp.concatenate([mask, mask, mask], axis=1) > 0.5
+                gate = jnp.where(image, gu_s[:, 2 * UNITS : 3 * UNITS], gu_s[:, :UNITS])
+                up = jnp.where(image, gu_s[:, 3 * UNITS :], gu_s[:, UNITS : 2 * UNITS])
+                act = gate / (1.0 + jnp.exp(-gate)) * up
+                both = jnp.concatenate(
+                    [jnp.where(image, 0.0, act), jnp.where(image, act, 0.0)], axis=1
+                ).astype(BF16)
+                ps_s[b % 2] = jnp.dot(both, wd_s[:, pl.ds(oth, HD)], preferred_element_type=F32)
+                swap(b).start()
+                own_s[b % 2] = jnp.dot(both, wd_s[:, pl.ds(own, HD)], preferred_element_type=F32)
+
+            @pl.when(b > 0)
+            def _():
+                done = b - 1
+                swap(done).wait()
+                ret_s[pl.ds(done * PER, PER)] = (
+                    (own_s[done % 2] + pr_s[done % 3]).astype(BF16).reshape(PER, CAP, HD)
+                )
+
+                @pl.loop(0, PER)
+                def _(i):
+                    n = done * PER + i
+
+                    @pl.when(n == 0)
+                    def _():
+                        pltpu.make_async_copy(ret_s.at[0], rin_s.at[0], rrecv.at[0]).start()
+
+                    @pl.when(n > 0)
+                    def _():
+                        pltpu.make_async_remote_copy(
+                            src_ref=ret_s.at[n],
+                            dst_ref=rin_s.at[n],
+                            send_sem=rsend,
+                            recv_sem=rrecv.at[done],
+                            device_id={"expert": chip_minus(me, n), "half": core},
+                            device_id_type=MESH,
+                        ).start()
 
             @pl.when(b + AHEAD < BATCHES)
             def _():
                 dispatch(b + AHEAD)
-
-            @pl.when(b < BATCHES - 1)
-            def _():
-                forward(b + 1)
-
 
     pl.run_scoped(
         experts,
@@ -273,7 +281,7 @@
         pltpu.VMEM((2 * UNITS, D), BF16),
         pltpu.VMEM((D, 2, 256), BF16),
         pltpu.VMEM((ROWS, 4 * UNITS), F32),
-        pltpu.VMEM((ROWS, HD), F32),
+        pltpu.VMEM((2, ROWS, HD), F32),
         pltpu.VMEM((CHIPS, CAP, 128), F32),
     )
 
@@ -530,8 +538,8 @@
             pltpu.VMEM((CHIPS, CAP, HD), BF16),
             pltpu.VMEM((CHIPS, CAP, HD), BF16),
             pltpu.VMEM((CHIPS, CAP, HD), BF16),
-            pltpu.VMEM((ROWS, HD), F32),
             pltpu.VMEM((2, ROWS, HD), F32),
+            pltpu.VMEM((3, ROWS, HD), F32),
             pltpu.VMEM((TOK, TOK), BF16),
             pltpu.VMEM((TOK, TOK), BF16),
             pltpu.VMEM((TOK, TOK), BF16),
@@ -547,8 +555,8 @@
             dma((BATCHES,)),
             dma((BATCHES,)),
             dma((BATCHES,)),
-            dma,
             dma((2,)),
+            dma((3,)),
             dma,
             dma((BATCHES,)),
             dma,

time: 155 us -> 148 us (0.955)
  Pallas kernels: 150 us -> 142 us
    pallas_call x1, Pallas kernels: 150 us -> 142 us  [layer_call(): pl.pallas_call(layer_kernel, out_shape=(jax.ShapeDtypeStruct((TOK, D), F3...]
where the time goes in v5:
time: 148 us; the launch traced here: 147 us
  Pallas kernels  142 us (96%)
  local copies, waits for them, and re-layouts  4.18 us (3%)
    pallas_call x1, Pallas kernels, layer_call(): pl.pallas_call(layer_kernel, out_shape=(jax.ShapeDtypeStruct((TOK, D), F3...  142 us
    unnamed x2, local copies, waits for them, and re-layouts  4.18 us

profile of v5, /device:TPU:0, one launch (start us, length us, event | category | flops | bytes accessed | tf_op | source)
XLA Modules:
  0.0 146.7 jit_solution(10759780225093796312)
XLA Ops:
  0.6 141.9 %shard_map.122 = (f32[128,2048]{1,0:T(8,128)}, bf16[128,2048]{1,0:T(8,128)(2,1)}) custom-call(bf16[128,2048]{1,0:T(8,128)(2,1)} %x_ref.1, s32[64,128]{1,0:T(8,128)} %bitcast.8, s32[8,128]{1,0:T(8,128)} %bitcast.10, f32[8,128]{1,0:T(8,128)} %bitcast.11, bf16[2,2048,2,384]{3,2,1,0:T(2,128)(2,1)} %wgu_hbm.1, bf16[768,2048]{1,0:T(8,128)(2,1)} %bitcast.7, ...), custom_call_target="tpu_custom_call" | custom-call | tf_op jit(solution)/shard_map/pallas_call | solution.py:529
  142.5 2.3 %copy.15 = f32[128,2048]{1,0:T(8,128)} copy(f32[128,2048]{1,0:T(8,128)} %get-tuple-element.4) | data formatting | bytes 2097152
  144.8 1.9 %copy.16 = bf16[128,2048]{1,0:T(8,128)(2,1)} copy(bf16[128,2048]{1,0:T(8,128)(2,1)} %get-tuple-element.5) | data formatting | bytes 1048576

commit v6 on v5

--- a/solution.py
+++ b/solution.py
@@ -59,7 +59,7 @@
 def layer_kernel(
     x_ref, mod_ref, ids_ref, rw_ref, wgu_hbm, wd_hbm, gain_ref, wq_hbm, wkv_hbm, qg_ref, kg_ref,
     ho_ref, att_ref,
-    kvw_s, out_s, a_s, b_s, ret_s, rin_s, ps_s, pr_s, val_s, hi_s, lo_s, valt_s, acc_s, nrm_s, q_s,
+    kvw_s, out_s, a_s, b_s, ret_s, rin_s, ps_s, pr_s, val_s, hi_s, lo_s, valt_s, q_s,
     buf0, buf1, buf2,
     wsem, dsend, drecv, fsend, frecv, psend, precv, rsend, rrecv, hsend, hrecv, ssem, rsem,
 ):
@@ -154,7 +154,7 @@
 
         @pl.loop(0, CHIPS)
         def _(n):
-            mask_s[n] = jnp.full((CAP, 128), mod_ref[chip_minus(me, n), 0], jnp.int32).astype(F32)
+            mask_s[n] = jnp.full((CAP, 128), mod_ref[chip_minus(me, n), 0], jnp.int32).astype(BF16)
 
         prow = lax.broadcasted_iota(jnp.int32, (256, 256), 0)
         pcol = lax.broadcasted_iota(jnp.int32, (256, 256), 1)
@@ -231,7 +231,7 @@
                         xa, w_s[pl.ds(own, HD), cols], preferred_element_type=F32
                     ) + jnp.dot(xb, w_s[pl.ds(oth, HD), cols], preferred_element_type=F32)
 
-                mask = mask_s[pl.ds(b * PER, PER)].reshape(ROWS, 128)
+                mask = mask_s[pl.ds(b * PER, PER)].reshape(ROWS, 128).astype(F32)
                 image = jnp.concatenate([mask, mask, mask], axis=1) > 0.5
                 gate = jnp.where(image, gu_s[:, 2 * UNITS : 3 * UNITS], gu_s[:, :UNITS])
                 up = jnp.where(image, gu_s[:, 3 * UNITS :], gu_s[:, UNITS : 2 * UNITS])
@@ -282,7 +282,7 @@
         pltpu.VMEM((D, 2, 256), BF16),
         pltpu.VMEM((ROWS, 4 * UNITS), F32),
         pltpu.VMEM((2, ROWS, HD), F32),
-        pltpu.VMEM((CHIPS, CAP, 128), F32),
+        pltpu.VMEM((CHIPS, CAP, 128), BF16),
     )
 
     def along(i, axis):
@@ -348,7 +348,7 @@
         scale = lax.rsqrt(jnp.mean(values * values, axis=-1, keepdims=True) + EPSILON)
         return (values * scale * gain).astype(BF16)
 
-    def project(wq_s):
+    def project(wq_s, acc_s, nrm_s):
         load = pltpu.make_async_copy(wq_hbm, wq_s, wsem.at[0])
         load.start()
         acc_s[...] = x_ref[:, pl.ds(own, HD)].astype(F32)
@@ -416,7 +416,9 @@
         ring(group(0), 2, 8)
         queries(5, 8)
 
-    pl.run_scoped(project, pltpu.VMEM((D, D), BF16))
+    pl.run_scoped(
+        project, pltpu.VMEM((D, D), BF16), pltpu.VMEM((TOK, HD), F32), pltpu.VMEM((TOK, D), BF16)
+    )
 
     pass_on(line, 1, 4)
     ring(group(1), 2, 12)
@@ -544,8 +546,6 @@
             pltpu.VMEM((TOK, TOK), BF16),
             pltpu.VMEM((TOK, TOK), BF16),
             pltpu.VMEM((TOK, TOK), BF16),
-            pltpu.VMEM((TOK, HD), F32),
-            pltpu.VMEM((TOK, D), BF16),
             pltpu.VMEM((2, 8 * TOK, 128), BF16),
         ]
         + [pltpu.VMEM((4, 4, 4, 4, rows, 128), BF16) for _, rows, _ in PARTS]
@@ -565,7 +565,7 @@
             dma((3, 24)),
         ],
         compiler_params=pltpu.CompilerParams(
-            collective_id=0, has_side_effects=True, vmem_limit_bytes=62 * 1024 * 1024
+            collective_id=0, has_side_effects=True, vmem_limit_bytes=54260000
         ),
     )(x, mod, ids, rw, wgu, wd, gain, wq, wkv, qg, kg)
 

time: 148 us -> 154 us (1.041)
  Pallas kernels: 142 us -> 146 us
  local copies, waits for them, and re-layouts: 4.18 us -> 6.94 us
    pallas_call x1, Pallas kernels: 142 us -> 146 us  [layer_call(): pl.pallas_call(layer_kernel, out_shape=(jax.ShapeDtypeStruct((TOK, D), F3...]
    unnamed x2 -> x16, local copies, waits for them, and re-layouts: 4.18 us -> 6.94 us
where the time goes in v6:
time: 154 us
  Pallas kernels  146 us (95%)
  local copies, waits for them, and re-layouts  6.94 us (5%)
    pallas_call x1, Pallas kernels, layer_call(): pl.pallas_call(layer_kernel, out_shape=(jax.ShapeDtypeStruct((TOK, D), F3...  146 us
    unnamed x16, local copies, waits for them, and re-layouts  6.94 us

profile of v6, /device:TPU:0, one launch (start us, length us, event | category | flops | bytes accessed | tf_op | source)
XLA Modules:
  0.0 154.1 jit_solution(177386564457348913)
XLA Ops:
  0.6 0.0 copy-start
  0.6 1.0 copy-done
  1.7 0.0 copy-start.1
  1.7 0.8 copy-done.1
  2.4 0.0 copy-start.2
  2.4 0.7 copy-done.2
  3.1 0.0 copy-start.3
  3.1 0.7 copy-done.3
  3.8 0.0 copy-start.4
  3.8 0.7 copy-done.4
  4.5 0.0 copy-start.5
  4.5 0.7 copy-done.5
  5.2 0.0 copy-start.6
  5.2 0.7 copy-done.6
  5.8 146.5 %shard_map.122 = (f32[128,2048]{1,0:T(8,128)S(1)}, bf16[128,2048]{1,0:T(8,128)(2,1)S(1)}) custom-call(bf16[128,2048]{1,0:T(8,128)(2,1)S(1)} %copy-done, s32[64,128]{1,0:T(8,128)S(1)} %bitcast.7, s32[8,128]{1,0:T(8,128)S(1)} %bitcast.9, f32[8,128]{1,0:T(8,128)S(1)} %bitcast.10, bf16[2,2048,2,384]{3,2,1,0:T(2,128)(2,1)} %wgu_hbm.1, ...), custom_call_target="tpu_custom_call" | custom-call | tf_op jit(solution)/shard_map/pallas_call | solution.py:531
  152.3 1.0 copy.15
  153.3 0.8 copy.16
Async XLA Ops:
  0.6 1.0 copy-start
  1.7 0.8 copy-start.1
  2.4 0.7 copy-start.2
  3.1 0.7 copy-start.3
  3.8 0.7 copy-start.4
  4.5 0.7 copy-start.5
  5.2 0.7 copy-start.6
